TPU v7x, 128 devices: a whole 4x4x4 slice. The times are simulated.
128 devices in a mesh: ctx: 16 (over x, z), ch: 8 (over y, core).
Axes of the slice: x: 4, y: 4, z: 4, core: 2. Of those that a mesh axis runs over, the one named last changes fastest.
Arguments:
- grad_out: float32 [16, 524288], P('ch', 'ctx'), may hold values from -6 to 6
- gate_in: float32 [16, 524288], P('ch', 'ctx'), may hold values from -6 to 6
- input_spectrum: float32 [2, 16, 32, 32768], P(None, 'ch', 'ctx'), may hold values from -6 to 6
- filter_spectrum: float32 [2, 4, 32, 32768], P(None, None, 'ctx'), may hold values from -6 to 6
Outputs:
- grad_input: float32 [16, 524288], P('ch', 'ctx')
- grad_gate: float32 [16, 524288], P('ch', 'ctx')
- grad_filter: float32 [4, 524288], P(None, 'ctx')
All inputs are finite; a program needn't handle non-finite values.
Results may differ from a plain program's by a relative error of at most 0.0003.
Values sent between devices are 32-bit elements; how exact they have to be, the bound alone decides.
A program may use at most 192 MiB of HBM per device.

v0:
```python
from functools import partial
import math

import jax
import jax.numpy as jnp
from jax import lax
from jax.sharding import PartitionSpec as P

CHANNELS = 16
FILTERS = 4
RADIX = 32
TILE = 256
COLS = 32768


contract = partial(jnp.einsum, precision=lax.Precision.HIGHEST)


def cut_along(x, dim, devices):
    dims = x.shape
    pieces = x.reshape(*dims[:dim], devices, dims[dim] // devices, *dims[dim + 1 :])
    return jnp.moveaxis(pieces, dim, 0)


def edges_of(length, count):
    lap = length // count
    if lap >= 8:
        lap -= lap % 8
    return [lap * k for k in range(1, count)]


def joined_along(pieces, dim):
    dims = list(pieces.shape[1:])
    dims[dim] *= pieces.shape[0]
    return jnp.moveaxis(pieces, 0, dim).reshape(dims)


def exchange_in_pieces(x, axis, pieces, split_dim, concat_dim):
    blocks = cut_along(x, split_dim, lax.axis_size(axis))
    cut = max(range(1, max(2, blocks.ndim - 1)), key=lambda d: blocks.shape[d])
    gathered = []
    for slab in jnp.split(blocks, edges_of(blocks.shape[cut], pieces), axis=cut):
        if slab.size:
            gathered.append(lax.all_to_all(slab, axis, split_axis=0, concat_axis=0, tiled=True))
    return joined_along(jnp.concatenate(gathered, axis=cut), concat_dim)


def from_everyone(x, axis):
    devices = lax.axis_size(axis)
    return lax.all_to_all(jnp.broadcast_to(x[None], (devices, *x.shape)), axis, 0, 0, tiled=True)


def of_everyone(x, axis):
    everything = from_everyone(x, axis)
    return jnp.sum(everything, axis=0)


def phases(counts, modulus):
    return (counts % modulus).astype(jnp.float32) * jnp.float32(2.0 * math.pi / modulus)


def complex_mul(left_real, left_imag, right_real, right_imag):
    return (
        left_real * right_real - left_imag * right_imag,
        left_real * right_imag + left_imag * right_real,
    )


def long_transform(real_part, imag_part, sign):
    leading = real_part.shape[:-1]
    half_tile = TILE // 2
    outer_index = jnp.arange(TILE, dtype=jnp.int32)
    inner_index = jnp.arange(half_tile, dtype=jnp.int32)
    outer_angle = phases(outer_index[:, None] * outer_index[None, :], TILE)
    outer_cos = jnp.cos(outer_angle)
    outer_sin = sign * jnp.sin(outer_angle)
    inner_angle = phases(inner_index[:, None] * inner_index[None, :], half_tile)
    inner_cos = jnp.cos(inner_angle)
    inner_sin = sign * jnp.sin(inner_angle)
    grid_real = real_part.reshape(leading + (TILE, half_tile))
    grid_imag = imag_part.reshape(leading + (TILE, half_tile))
    first_real = contract("cb,...ba->...ca", outer_cos, grid_real) - contract(
        "cb,...ba->...ca", outer_sin, grid_imag
    )
    first_imag = contract("cb,...ba->...ca", outer_cos, grid_imag) + contract(
        "cb,...ba->...ca", outer_sin, grid_real
    )
    twist = phases(outer_index[:, None] * inner_index[None, :], TILE * half_tile)
    first_real, first_imag = complex_mul(
        first_real, first_imag, jnp.cos(twist), sign * jnp.sin(twist)
    )
    second_real = contract("...ca,ad->...dc", first_real, inner_cos) - contract(
        "...ca,ad->...dc", first_imag, inner_sin
    )
    second_imag = contract("...ca,ad->...dc", first_imag, inner_cos) + contract(
        "...ca,ad->...dc", first_real, inner_sin
    )
    return (
        second_real.reshape(leading + (TILE * half_tile,)),
        second_imag.reshape(leading + (TILE * half_tile,)),
    )


def per_device(grad_out, gate_in, input_spectrum, filter_spectrum):
    shards = lax.axis_size("ctx")
    position = lax.axis_index("ctx")
    column_slab = COLS // shards
    freq_rows = RADIX // shards
    time_rows = RADIX // 2 // shards
    channels = grad_out.shape[0]
    total = RADIX * COLS
    scale = jnp.float32(total ** (-0.5))
    filter_index = lax.axis_index("ch") * channels // (CHANNELS // FILTERS)
    gated_grad = grad_out * gate_in
    blocks = gated_grad.reshape(channels, time_rows, COLS)
    slabs = lax.all_to_all(blocks, "ctx", split_axis=2, concat_axis=1, tiled=True)
    radix_index = jnp.arange(RADIX, dtype=jnp.int32)
    half_index = jnp.arange(RADIX // 2, dtype=jnp.int32)
    radix_phase = phases(radix_index[:, None] * half_index[None, :], RADIX)
    spread_real = contract("kj,cjs->cks", jnp.cos(radix_phase), slabs)
    spread_imag = contract("kj,cjs->cks", -jnp.sin(radix_phase), slabs)
    slab_cols = position * column_slab + jnp.arange(column_slab, dtype=jnp.int32)
    twist = phases(radix_index[:, None] * slab_cols[None, :], total)
    spread_real, spread_imag = complex_mul(
        spread_real, spread_imag, jnp.cos(twist), -jnp.sin(twist)
    )
    rows_moved = lax.all_to_all(
        jnp.stack([spread_real, spread_imag]), "ctx", split_axis=2, concat_axis=3, tiled=True
    )
    gated_real, gated_imag = long_transform(rows_moved[0], rows_moved[1], -1.0)
    gated_real = gated_real * scale
    gated_imag = gated_imag * scale
    in_real = input_spectrum[0]
    in_imag = input_spectrum[1]
    chosen = lax.dynamic_index_in_dim(filter_spectrum, filter_index, axis=1, keepdims=False)
    filt_real = chosen[0][None]
    filt_imag = chosen[1][None]
    conv_real, conv_imag = complex_mul(in_real, in_imag, filt_real, filt_imag)
    input_real, input_imag = complex_mul(filt_real, -filt_imag, gated_real, gated_imag)
    weight_real, weight_imag = complex_mul(in_real, -in_imag, gated_real, gated_imag)
    stacked_real = jnp.concatenate([conv_real, input_real, weight_real])
    stacked_imag = jnp.concatenate([conv_imag, input_imag, weight_imag])
    inv_real, inv_imag = long_transform(stacked_real, stacked_imag, 1.0)
    freq_ids = position * freq_rows + jnp.arange(freq_rows, dtype=jnp.int32)
    col_ids = jnp.arange(COLS, dtype=jnp.int32)
    back_phase = phases(freq_ids[:, None] * col_ids[None, :], total)
    inv_real, inv_imag = complex_mul(inv_real, inv_imag, jnp.cos(back_phase), jnp.sin(back_phase))
    gathered = exchange_in_pieces(jnp.stack([inv_real, inv_imag]), "ctx", 2, 3, 2)
    out_phase = phases(half_index[:, None] * radix_index[None, :], RADIX)
    signal = contract("jk,rks->rjs", jnp.cos(out_phase), gathered[0]) - contract(
        "jk,rks->rjs", jnp.sin(out_phase), gathered[1]
    )
    signal = signal * scale
    restored = lax.all_to_all(signal, "ctx", split_axis=1, concat_axis=2, tiled=True)
    restored = restored.reshape(restored.shape[0], -1)
    conv = restored[:channels]
    grad_gate = grad_out * conv
    grad_input = restored[channels : 2 * channels]
    filter_terms = restored[2 * channels :]
    filter_terms = jnp.sum(filter_terms, axis=0, keepdims=True)
    selector = (jnp.arange(FILTERS, dtype=jnp.int32) == filter_index).astype(jnp.float32)
    placed = selector[:, None] * filter_terms
    grad_filter = of_everyone(placed, "ch")
    return (grad_input, grad_gate, grad_filter)


def solution(mesh):
    return jax.shard_map(
        per_device,
        mesh=mesh,
        in_specs=(
            P("ch", "ctx"),
            P("ch", "ctx"),
            P(None, "ch", "ctx", None),
            P(None, None, "ctx", None),
        ),
        out_specs=(P("ch", "ctx"), P("ch", "ctx"), P(None, "ctx")),
        check_vma=False,
    )
```

profile of v0, /device:TPU:1, one launch (start us, length us, event | category | flops | bytes accessed | tf_op | source)
XLA Modules:
  0.0 464.7 jit_solution(8174818476619542475)
XLA Ops:
  0.6 1.2 multiply_bitcast_fusion
  1.8 23.9 %copy.187 = f32[2,1,32768]{0,1,2:T(1,128)} copy(f32[2,1,32768]{2,0,1:T(2,128)S(1)} %multiply_bitcast_fusion) | data formatting | bytes 524288 | tf_op jit(solution)/shard_map/reshape | solution.py:115
  26.3 146.5 %reduce.1 = f32[32768,2]{1,0:T(8,128)} reduce(f32[32768,1,2]{2,1,0:T(1,128)} %bitcast.157, f32[]{:T(128)} %broadcast.519), dimensions={1}, to_apply=%bitcast.142.reduce_sub_computation | reduce | bytes 524292
  172.8 14.4 %reshape.365 = f32[16,1,4096]{2,1,0:T(1,128)} reshape(f32[32768,2]{1,0:T(8,128)} %reduce.1) | data formatting | bytes 524288
  187.2 8.8 %all-to-all-start = ((f32[16,1,4096]{2,1,0:T(1,128)}), f32[16,1,4096]{2,1,0:T(1,128)S(1)}, u32[]{:S(2)}, u32[]{:S(2)}) async-start(f32[16,1,4096]{2,1,0:T(1,128)} %reshape.365), calls=%async_computation | async-start | bytes 524288 | tf_op jit(solution)/shard_map/all_to_all | solution.py:116
  197.1 1.0 fusion.62
  198.2 0.9 fusion.212
  199.1 1.1 dynamic-slice_bitcast_fusion.1
  200.2 3.3 all-to-all-done
  203.5 1.3 reduce.2
  204.7 29.8 %reshape.366 = f32[32768,1,2]{2,1,0:T(1,128)} reshape(f32[16,4096]{1,0:T(8,128)S(1)} %reduce.2) | data formatting | bytes 524288
  234.6 10.0 %copy.240 = f32[2,16,2048]{2,1,0:T(8,128)S(1)} copy(f32[2,16,2048]{0,2,1:T(8,128)} %bitcast.158) | data formatting | bytes 524288 | tf_op jit(solution)/shard_map/all_to_all | solution.py:116
  246.1 1.8 copy.189
  247.9 3.7 all-to-all-start.1
  251.8 1.5 squeeze.14
  253.3 1.0 copy.184
  254.8 1.0 copy.186
  256.5 2.1 fusion.47
  258.6 7.9 %all-to-all-done.1 = f32[2,2,32,2048]{3,1,0,2:T(2,128)S(1)} async-done(((f32[2,2,32,2048]{3,1,0,2:T(2,128)}), f32[2,2,32,2048]{3,1,0,2:T(2,128)S(1)}, u32[]{:S(2)}, u32[]{:S(2)}) %all-to-all-start.1) | async-done | bytes 1048608 | tf_op jit(solution)/shard_map/all_to_all | solution.py:127
  267.3 1.8 fusion.33
  269.2 1.8 fusion.31
  271.1 1.8 fusion.7
  272.9 1.8 fusion.6
  274.7 0.9 fusion.73
  275.6 0.9 fusion.75
  276.5 1.7 fusion.4
  278.2 1.9 reshape.352
  280.1 1.2 copy.202
  281.3 1.7 fusion.5
  283.1 1.2 reshape.351
  284.2 1.2 copy.198
  285.4 1.5 multiply_subtract_fusion.4
  287.0 2.4 fusion.9
  289.4 2.4 fusion.8
  291.8 2.4 convolution_subtract_fusion.1
  294.2 2.4 convolution_add_fusion
  296.7 2.2 fusion.14
  298.8 2.9 fusion.10
  301.7 3.0 subtract_bitcast_fusion
  304.8 2.6 reshape.353
  307.3 4.3 add_bitcast_fusion
  311.6 1.6 reshape.354
  313.5 1.4 multiply_subtract_fusion
  315.2 1.4 fusion.211
  316.7 2.3 copy.216
  319.0 4.2 all-to-all-start.2
  323.2 2.6 copy.217
  325.9 17.6 %all-to-all-done.2 = f32[16,2,3,2,2048]{4,3,2,1,0:T(2,128)S(1)} async-done(((f32[16,2,3,2,2048]{4,3,2,1,0:T(2,128)}), f32[16,2,3,2,2048]{4,3,2,1,0:T(2,128)S(1)}, u32[]{:S(2)}, u32[]{:S(2)}) %all-to-all-start.2) | async-done | bytes 1572896 | tf_op jit(solution)/shard_map/all_to_all | solution.py:44
  343.5 25.6 %all_to_all.51 = f32[16,2,3,2,2048]{4,3,2,1,0:T(2,128)S(1)} all-to-all(f32[16,2,3,2,2048]{4,3,2,1,0:T(2,128)S(1)} %copy.217), channel_id=1, replica_groups=mesh['ctx'=16,'ch'=8] {'ctx'}, dimensions={0} | all-to-all | bytes 3145728 | tf_op jit(solution)/shard_map/all_to_all | solution.py:44
  369.1 2.3 maximum_bitcast_fusion.1
  371.4 2.5 fusion.210
  374.1 1.1 squeeze.16
  375.2 1.9 fusion.103
  377.3 1.1 squeeze.17
  378.3 2.1 fusion.1
  380.5 1.5 copy.220
  381.9 3.7 all-to-all-start.4
  385.6 13.7 %all-to-all-done.4 = f32[6,16,2048]{2,0,1:T(8,128)S(1)} async-done(((f32[6,16,2048]{2,0,1:T(8,128)}), f32[6,16,2048]{2,0,1:T(8,128)S(1)}, u32[]{:S(2)}, u32[]{:S(2)}) %all-to-all-start.4) | async-done | bytes 786464 | tf_op jit(solution)/shard_map/all_to_all | solution.py:154
  399.4 1.0 slice_reduce_fusion
  400.5 2.5 broadcast_in_dim.2
  403.1 8.9 %all-to-all-start.5 = ((f32[8,4,32768]{2,1,0:T(4,128)}), f32[8,4,32768]{2,1,0:T(4,128)}, u32[]{:S(2)}, u32[]{:S(2)}) async-start(f32[8,4,32768]{2,1,0:T(4,128)} %broadcast_in_dim.2), calls=%async_computation.5 | async-start | bytes 8388608 | tf_op jit(solution)/shard_map/all_to_all | solution.py:50
  412.0 0.8 mul.810
  412.9 47.9 %all-to-all-done.5 = f32[8,4,32768]{2,1,0:T(4,128)} async-done(((f32[8,4,32768]{2,1,0:T(4,128)}), f32[8,4,32768]{2,1,0:T(4,128)}, u32[]{:S(2)}, u32[]{:S(2)}) %all-to-all-start.5) | async-done | bytes 4194336 | tf_op jit(solution)/shard_map/all_to_all | solution.py:50
  460.8 3.7 reduce_sum.19
  (39 shorter events, 6.5 us)
Async XLA Ops:
  187.2 11.0 %copy-start.5 = (f32[2,2,2,32768]{3,2,1,0:T(2,128)S(1)}, f32[2,2,2,32768]{3,2,1,0:T(2,128)}, u32[]{:S(2)}) copy-start(f32[2,2,2,32768]{3,2,1,0:T(2,128)} %param.6) | copy-start | bytes 3145732
  187.2 16.3 %all-to-all-start = ((f32[16,1,4096]{2,1,0:T(1,128)}), f32[16,1,4096]{2,1,0:T(1,128)S(1)}, u32[]{:S(2)}, u32[]{:S(2)}) async-start(f32[16,1,4096]{2,1,0:T(1,128)} %reshape.365), calls=%async_computation | async-start | bytes 524288 | tf_op jit(solution)/shard_map/all_to_all | solution.py:116
  247.9 18.7 %all-to-all-start.1 = ((f32[2,2,32,2048]{3,1,0,2:T(2,128)}), f32[2,2,32,2048]{3,1,0,2:T(2,128)S(1)}, u32[]{:S(2)}, u32[]{:S(2)}) async-start(f32[2,2,32,2048]{3,1,0,2:T(2,128)} %copy.189), calls=%async_computation.1 | async-start | bytes 2097152 | tf_op jit(solution)/shard_map/all_to_all | solution.py:127
  283.1 2.4 copy-start.2
  283.1 2.4 copy-start.3
  311.6 1.9 copy-start.1
  311.6 1.9 copy-start.6
  319.0 24.4 %all-to-all-start.2 = ((f32[16,2,3,2,2048]{4,3,2,1,0:T(2,128)}), f32[16,2,3,2,2048]{4,3,2,1,0:T(2,128)S(1)}, u32[]{:S(2)}, u32[]{:S(2)}) async-start(f32[16,2,3,2,2048]{4,3,2,1,0:T(2,128)} %copy.216), calls=%async_computation.2 | async-start | bytes 3145728 | tf_op jit(solution)/shard_map/all_to_all | solution.py:44
  375.2 1.9 copy-start
  381.9 17.4 %all-to-all-start.4 = ((f32[6,16,2048]{2,0,1:T(8,128)}), f32[6,16,2048]{2,0,1:T(8,128)S(1)}, u32[]{:S(2)}, u32[]{:S(2)}) async-start(f32[6,16,2048]{2,0,1:T(8,128)} %copy.220), calls=%async_computation.4 | async-start | bytes 2097152 | tf_op jit(solution)/shard_map/all_to_all | solution.py:154
  403.1 9.0 %copy-start.4 = (f32[2,32768]{1,0:T(2,128)S(1)}, f32[2,32768]{1,0:T(2,128)}, u32[]{:S(2)}) copy-start(f32[2,32768]{1,0:T(2,128)} %param.4) | copy-start | bytes 786436
  403.1 57.7 %all-to-all-start.5 = ((f32[8,4,32768]{2,1,0:T(4,128)}), f32[8,4,32768]{2,1,0:T(4,128)}, u32[]{:S(2)}, u32[]{:S(2)}) async-start(f32[8,4,32768]{2,1,0:T(4,128)} %broadcast_in_dim.2), calls=%async_computation.5 | async-start | bytes 8388608 | tf_op jit(solution)/shard_map/all_to_all | solution.py:50
where the time goes:
time: 471 us; the launch traced here: 465 us
  other arithmetic  165 us (35%)
  local copies, waits for them, and re-layouts  113 us (24%)
  waiting for transfers between devices  90.5 us (19%)
  matrix products  40 us (8%)
  starting transfers between devices  29.3 us (6%)
  blocking collectives  25.6 us (5%)
    unnamed x1, other arithmetic  147 us
    all_to_all x1, waiting for transfers between devices, from_everyone(): lax.all_to_all(jnp.broadcast_to(x[None], (devices, *x.shape)), axis, 0, 0...  47.9 us
    unnamed x19, local copies, waits for them, and re-layouts  46.1 us
    all_to_all x1, blocking collectives, exchange_in_pieces(): lax.all_to_all(slab, axis, split_axis=0, concat_axis=0, tiled=True)  25.6 us
    reshape x1, local copies, waits for them, and re-layouts, per_device(): blocks = gated_grad.reshape(channels, time_rows, COLS)  23.9 us
    all_to_all x1, waiting for transfers between devices, exchange_in_pieces(): lax.all_to_all(slab, axis, split_axis=0, concat_axis=0, tiled=True)  17.6 us
    all_to_all x1, waiting for transfers between devices, per_device(): lax.all_to_all(signal, 'ctx', split_axis=1, concat_axis=2, tiled=True)  13.7 us
    all_to_all x1, local copies, waits for them, and re-layouts, per_device(): lax.all_to_all(blocks, 'ctx', split_axis=2, concat_axis=1, tiled=True)  9.97 us
  transfers between devices with their start and end apart: 5, of which 5 were waited for; matrix products, arithmetic and copies ran while one was open for 3% of the time, Pallas kernels for 0%

commit v1 on v0

v1 whole, which is shorter than its diff:
```python
from functools import partial
import math

import jax
import jax.numpy as jnp
import numpy as np
from jax import lax
from jax.experimental import pallas as pl
from jax.experimental.pallas import tpu as pltpu
from jax.sharding import PartitionSpec as P

CHANNELS = 16
FILTERS = 4
RADIX = 32
COLS = 32768
TOTAL = RADIX * COLS
SHARDS = 16
WIDE = 256
LANES = 128
MESH = pl.DeviceIdType.MESH
F32 = jnp.float32
BF16 = jnp.bfloat16


def real_form(matrix):
    return np.block([[matrix.real, -matrix.imag], [matrix.imag, matrix.real]])


def halves(matrix):
    whole = matrix.astype(np.float32)
    high = whole.astype(jnp.bfloat16)
    low = (matrix - high.astype(np.float64)).astype(np.float32).astype(jnp.bfloat16)
    return np.stack([high, low])


def tables():
    def unit(counts, modulus):
        return np.exp(-2j * np.pi * (counts % modulus) / modulus)

    wide = np.arange(WIDE)
    lanes = np.arange(LANES)
    rows = np.arange(RADIX)
    dft_wide = unit(wide[:, None] * wide[None, :], WIDE)
    dft_lanes = unit(lanes[:, None] * lanes[None, :], LANES)
    inner = unit(wide[:, None] * lanes[None, :], COLS) * 2.0**-10
    lane_rows = unit(rows[:, None] * lanes[None, :], TOTAL)
    wide_rows = unit(wide[:, None] * rows[None, :], TOTAL // LANES)
    picked = np.concatenate([wide_rows.real, wide_rows.imag, np.zeros((WIDE, LANES - 2 * RADIX))], axis=1)
    return (
        np.stack([halves(real_form(dft_wide)), halves(real_form(dft_wide.conj()))]),
        np.stack([halves(real_form(dft_lanes)), halves(real_form(dft_lanes.conj()))]),
        np.stack([inner.real, inner.imag]).astype(np.float32),
        np.stack([lane_rows.real, lane_rows.imag]).astype(np.float32),
        picked.astype(np.float32),
    )


def times_unit(value, turn):
    re, im = value
    turn = turn % 1.0
    if turn == 0.0:
        return re, im
    if turn == 0.5:
        return negated(re), negated(im)
    if turn == 0.25:
        return negated(im), re
    if turn == 0.75:
        return im, negated(re)
    c, s = math.cos(2 * math.pi * turn), math.sin(2 * math.pi * turn)
    if im is None:
        return re * c, re * s
    if re is None:
        return im * (-s), im * c
    if turn in (0.125, 0.375, 0.625, 0.875):
        h = math.sqrt(0.5)
        if turn == 0.125:
            return (re - im) * h, (re + im) * h
        if turn == 0.375:
            return (re + im) * (-h), (re - im) * h
        if turn == 0.625:
            return (im - re) * h, (re + im) * (-h)
        return (re + im) * h, (im - re) * h
    return re * c - im * s, re * s + im * c


def negated(x):
    return None if x is None else -x


def plus(a, b):
    if a is None:
        return b
    return a if b is None else a + b


def minus(a, b):
    if b is None:
        return a
    return -b if a is None else a - b


def real_dft(xs):
    n = len(xs)
    if n == 1:
        return [(xs[0], None)]
    even, odd = real_dft(xs[0::2]), real_dft(xs[1::2])
    if n == 2:
        a, b = even[0][0], odd[0][0]
        return [(plus(a, b), None), (minus(a, b), None)]
    out = [None] * (n // 2 + 1)
    for k in range(n // 4 + 1):
        e, t = even[k], times_unit(odd[k], -k / n)
        out[k] = (plus(e[0], t[0]), plus(e[1], t[1]))
        if n // 2 - k != k:
            out[n // 2 - k] = (minus(e[0], t[0]), minus(t[1], e[1]))
    return out


def back_dft(xs, first_half=False):
    n = len(xs)
    if n == 1:
        return list(xs)
    even, odd = back_dft(xs[0::2]), back_dft(xs[1::2])
    upper, lower = [], []
    for k in range(n // 2):
        e, t = even[k], times_unit(odd[k], k / n)
        upper.append((e[0] + t[0], e[1] + t[1]))
        if not first_half:
            lower.append((e[0] - t[0], e[1] - t[1]))
    return upper + lower


def parts(x):
    high = x.astype(BF16)
    return high, (x - high.astype(F32)).astype(BF16)


def product(left, x, nt=False):
    high, low = parts(x)
    dims = (((1,), (1 if nt else 0,)), ((), ()))
    dot = partial(lax.dot_general, dimension_numbers=dims, preferred_element_type=F32)
    return dot(left[0], high) + (dot(left[0], low) + dot(left[1], high))


def kernel(
    grad_hbm, gate_hbm, spec_hbm, filt_hbm, wide_hbm, lanes_hbm, inner_hbm, lane_rows_hbm, picked_hbm,
    gi_hbm, gg_hbm, gf_hbm,
    grad, gate, spec, filt, wide, lanes, inner, lane_rows, picked,
    pre, mid, midt,
    x_out, x_in, y_out, y_in, c_out, c_in, i_out, i_in, d_out, d_in, e_out, e_in,
    prods, fsum, fpart, f_out, f_in, g_out, g_in, g_all, gf,
    load_sem, send_sem, recv_sem,
):
    me = lax.axis_index("ctx")
    group = lax.axis_index("ch")
    core = group % 2
    plane = group // 2
    other = group + 1 - 2 * core

    def load(k, src, dst):
        copy = pltpu.make_async_copy(src, dst, load_sem.at[k])
        copy.start()
        return copy

    loads = [
        load(0, grad_hbm, grad),
        load(1, gate_hbm, gate),
        load(2, inner_hbm, inner),
        load(3, lane_rows_hbm, lane_rows),
        load(4, picked_hbm, picked),
        load(5, spec_hbm, spec),
        load(6, filt_hbm.at[:, plane], filt),
        load(7, lanes_hbm, lanes),
        load(8, wide_hbm, wide),
    ]

    barrier = pltpu.get_barrier_semaphore()
    pl.semaphore_signal(barrier, inc=1, device_id={"ch": other}, device_id_type=MESH)
    for step in range(1, SHARDS):
        peer = (me + step) % SHARDS
        pl.semaphore_signal(barrier, inc=1, device_id={"ctx": peer}, device_id_type=MESH)
        pl.semaphore_signal(barrier, inc=1, device_id={"ctx": peer, "ch": other}, device_id_type=MESH)
    for step in range(1, 4):
        for side in range(2):
            there = 2 * ((plane + step) % 4) + side
            pl.semaphore_signal(barrier, inc=1, device_id={"ch": there}, device_id_type=MESH)
    pl.semaphore_wait(barrier, 2 * SHARDS - 1 + 6)

    def send_all(k, out, into):
        for step in range(1, SHARDS):
            peer = (me + step) % SHARDS
            pltpu.make_async_remote_copy(
                out.at[peer], into.at[me], send_sem.at[k], recv_sem.at[k],
                device_id={"ctx": peer}, device_id_type=MESH,
            ).start()
        into[me] = out[me]

    def bulk(k, ref):
        return pltpu.make_async_remote_copy(
            ref, ref, send_sem.at[k], recv_sem.at[k], device_id={"ctx": (me + 1) % SHARDS}, device_id_type=MESH
        )

    def arrived(k, into):
        bulk(k, into.at[pl.ds(0, SHARDS - 1)]).wait_recv()

    def left(k, out):
        bulk(k, out.at[pl.ds(0, SHARDS - 1)]).wait_send()

    loads[0].wait()
    loads[1].wait()
    x_out[...] = (grad[...] * gate[...]).reshape(SHARDS, 32, LANES)
    send_all(0, x_out, x_in)

    for k in (2, 3, 4):
        loads[k].wait()
    lane_ids = lax.broadcasted_iota(jnp.int32, (WIDE, LANES), 1)
    for b in range(2):
        row = 2 * me + b
        for ri in range(2):
            column = jnp.sum(jnp.where(lane_ids == row + RADIX * ri, picked[...], 0.0), axis=1, keepdims=True)
            pre[b, ri] = jnp.broadcast_to(column, (WIDE, LANES))
        vr = lane_rows[0, pl.ds(row, 1), :]
        vi = lane_rows[1, pl.ds(row, 1), :]
        tr = inner[0] * vr - inner[1] * vi
        ti = inner[0] * vi + inner[1] * vr
        mid[b, 0] = tr
        mid[b, 1] = ti
        midt[b, 0] = tr.T * 0.5
        midt[b, 1] = ti.T * 0.5

    for k in (5, 6, 7, 8):
        loads[k].wait()

    def spread(ref, b):
        return jnp.concatenate([ref[pl.ds(2 * s + b, LANES, stride=4), :] for s in range(2)], axis=1)

    def inverse_rows(b, arrays):
        mr, mi = midt[b, 0], midt[b, 1]
        stacked = []
        for re, im in arrays:
            c = product(lanes[1], jnp.concatenate([re, im], axis=0))
            cr, ci = c[:LANES], c[LANES:]
            stacked.append(jnp.concatenate([cr * mr + ci * mi, ci * mr - cr * mi], axis=1))
        t = product(wide[1], jnp.concatenate(stacked, axis=0) if len(stacked) > 1 else stacked[0], nt=True)
        pr, pi = pre[b, 0], pre[b, 1]
        out = []
        for k in range(len(arrays)):
            sr = t[:WIDE, LANES * k : LANES * (k + 1)]
            si = t[WIDE:, LANES * k : LANES * (k + 1)]
            out.append((sr * pr + si * pi, si * pr - sr * pi))
        return out

    def fill(out, b, arrays):
        for ch, (re, im) in enumerate(inverse_rows(b, arrays)):
            out[:, b, 0, ch] = re.reshape(SHARDS, 16, LANES)
            out[:, b, 1, ch] = im.reshape(SHARDS, 16, LANES)

    for b in range(2):
        hr, hi = spread(filt.at[0], b), spread(filt.at[1], b)
        prods[b, 0, 0], prods[b, 0, 1] = hr, hi
        for ch in range(2):
            ur, ui = spread(spec.at[0, ch], b), spread(spec.at[1, ch], b)
            prods[b, 1 + ch, 0], prods[b, 1 + ch, 1] = ur, ui

    def conv_row(b, carry):
        hr, hi = prods[b, 0, 0], prods[b, 0, 1]
        arrays = []
        for ch in range(2):
            ur, ui = prods[b, 1 + ch, 0], prods[b, 1 + ch, 1]
            arrays.append((ur * hr - ui * hi, ur * hi + ui * hr))
        fill(c_out, b, arrays)
        return carry

    arrived(0, x_in)

    def slab_forward(step, carry):
        ch, half = step // 2, step % 2
        xs = [x_in[j, pl.ds(16 * half + ch, 8, stride=2), :] for j in range(SHARDS)]
        ys = real_dft(xs + [None] * SHARDS)
        at = pl.ds(pl.multiple_of(8 * half, 8), 8)
        for r in range(RADIX):
            re, im = ys[min(r, RADIX - r)]
            if im is None:
                im = jnp.zeros_like(re)
            elif r > RADIX // 2:
                im = -im
            y_out[r // 2, r % 2, 0, ch, at, :] = re
            y_out[r // 2, r % 2, 1, ch, at, :] = im
        return carry

    lax.fori_loop(0, 4, slab_forward, 0)
    send_all(1, y_out, y_in)

    lax.fori_loop(0, 2, conv_row, 0)
    send_all(2, c_out, c_in)

    arrived(1, y_in)

    def forward_row(b, carry):
        pr = jnp.concatenate([pre[b, 0]] * 2, axis=1)
        pi = jnp.concatenate([pre[b, 1]] * 2, axis=1)
        yr = jnp.concatenate([y_in[:, b, 0, ch].reshape(WIDE, LANES) for ch in range(2)], axis=1)
        yi = jnp.concatenate([y_in[:, b, 1, ch].reshape(WIDE, LANES) for ch in range(2)], axis=1)
        a = product(wide[0], jnp.concatenate([yr * pr - yi * pi, yr * pi + yi * pr], axis=0))
        mr, mi = mid[b, 0], mid[b, 1]
        fr = fi = None
        for ch in range(2):
            ar = a[:WIDE, LANES * ch : LANES * (ch + 1)]
            ai = a[WIDE:, LANES * ch : LANES * (ch + 1)]
            g = product(lanes[0], jnp.concatenate([ar * mr - ai * mi, ar * mi + ai * mr], axis=1), nt=True)
            gr, gi = g[:LANES], g[LANES:]
            ur, ui = prods[b, 1 + ch, 0], prods[b, 1 + ch, 1]
            wr, wi = ur * gr + ui * gi, ur * gi - ui * gr
            fr, fi = (wr, wi) if ch == 0 else (fr + wr, fi + wi)
            hr, hi = prods[b, 0, 0], prods[b, 0, 1]
            prods[b, 1 + ch, 0], prods[b, 1 + ch, 1] = hr * gr + hi * gi, hr * gi - hi * gr
        fsum[b, 0], fsum[b, 1] = fr, fi
        return carry

    lax.fori_loop(0, 2, forward_row, 0)

    swap = pltpu.make_async_remote_copy(
        fsum.at[1 - core], fpart, send_sem.at[3], recv_sem.at[3], device_id={"ch": other}, device_id_type=MESH
    )
    swap.start()

    def input_row(b, carry):
        fill(i_out, b, [(prods[b, 1 + ch, 0], prods[b, 1 + ch, 1]) for ch in range(2)])
        return carry

    swap.wait_recv()
    ((re, im),) = inverse_rows(core, [(fsum[core, 0] + fpart[0], fsum[core, 1] + fpart[1])])
    f_out[:, 0] = re.reshape(2 * SHARDS, 8, LANES)
    f_out[:, 1] = im.reshape(2 * SHARDS, 8, LANES)
    for step in range(SHARDS):
        peer = (me + step) % SHARDS
        for side in range(2):
            if step == 0 and side == 0:
                continue
            there = other if side else group
            half = 1 - core if side else core
            pltpu.make_async_remote_copy(
                f_out.at[2 * peer + half], f_in.at[2 * me + core], send_sem.at[4], recv_sem.at[4],
                device_id={"ctx": peer, "ch": there}, device_id_type=MESH,
            ).start()
    f_in[2 * me + core] = f_out[2 * me + core]

    lax.fori_loop(0, 2, input_row, 0)
    send_all(5, i_out, i_in)

    def slab_back(src, out):
        def body(half, carry):
            at = pl.ds(pl.multiple_of(8 * half, 8), 8)

            def row(r, ri, ch):
                return src[r // 2, r % 2, ri, ch, at, :]

            ws = [None] * RADIX
            for r in range(RADIX // 2 + 1):
                q = (RADIX - r) % RADIX
                a = row(r, 0, 0) + row(q, 0, 0)
                c = row(r, 0, 1) + row(q, 0, 1)
                if q == r:
                    ws[r] = (a, c)
                    continue
                bb = row(r, 1, 0) - row(q, 1, 0)
                d = row(r, 1, 1) - row(q, 1, 1)
                ws[r] = (a - d, bb + c)
                ws[q] = (a + d, c - bb)
            for j, (re, im) in enumerate(back_dft(ws, first_half=True)):
                out[j, pl.ds(16 * half, 8, stride=2), :] = re
                out[j, pl.ds(16 * half + 1, 8, stride=2), :] = im
            return carry

        lax.fori_loop(0, 2, body, 0)

    arrived(2, c_in)
    slab_back(c_in, d_out)
    send_all(6, d_out, d_in)

    bulk(4, f_in.at[pl.ds(0, 2 * SHARDS - 1)]).wait_recv()
    ws = [(f_in[r, 0], f_in[r, 1]) for r in range(RADIX)]
    for j, (re, _) in enumerate(back_dft(ws, first_half=True)):
        g_out[j] = re + re
    send_all(7, g_out, g_in)

    arrived(5, i_in)
    slab_back(i_in, e_out)
    send_all(8, e_out, e_in)

    arrived(7, g_in)
    for step in range(4):
        for side in range(2):
            if step == 0 and side == 0:
                continue
            there = 2 * ((plane + step) % 4) + (1 - core if side else core)
            pltpu.make_async_remote_copy(
                g_in, g_all.at[group], send_sem.at[9], recv_sem.at[9],
                device_id={"ch": there}, device_id_type=MESH,
            ).start()
    g_all[group] = g_in[...]

    arrived(6, d_in)
    gate[...] = grad[...] * d_in[...].reshape(512, LANES)
    store_gg = load(1, gate, gg_hbm)
    arrived(8, e_in)
    store_gi = load(0, e_in, gi_hbm)
    bulk(9, g_all.at[pl.ds(0, 7)]).wait_recv()
    for f in range(FILTERS):
        for c in range(2):
            for q in range(SHARDS):
                gf[pl.ds(64 * q + 32 * c + f, 8, stride=4), :] = g_all[2 * f + c, q]
    store_gf = load(2, gf, gf_hbm)

    left(0, x_out)
    left(1, y_out)
    left(2, c_out)
    swap.wait_send()
    bulk(4, f_out.at[pl.ds(0, 2 * SHARDS - 1)]).wait_send()
    left(5, i_out)
    left(6, d_out)
    left(7, g_out)
    left(8, e_out)
    bulk(9, g_all.at[pl.ds(0, 7)]).wait_send()
    store_gg.wait()
    store_gi.wait()
    store_gf.wait()


def per_device(grad_out, gate_in, input_spectrum, filter_spectrum):
    def tiled(x):
        lead = x.shape[:-2]
        pieces = x.reshape(*lead, x.shape[-2], WIDE, LANES)
        return jnp.swapaxes(pieces, -3, -2).reshape(*lead, WIDE * x.shape[-2], LANES)

    def untiled(x, rows):
        return jnp.swapaxes(x.reshape(WIDE, rows, LANES), 0, 1).reshape(rows, COLS)

    consts = tables()
    operands = (tiled(grad_out), tiled(gate_in), tiled(input_spectrum), tiled(filter_spectrum), *consts)
    slab = lambda *dims: pltpu.VMEM((SHARDS, *dims, LANES), F32)
    wave = slab(2, 2, 2, 16)
    scratch = [
        pltpu.VMEM((512, LANES), F32),
        pltpu.VMEM((512, LANES), F32),
        pltpu.VMEM((2, 2, 512, LANES), F32),
        pltpu.VMEM((2, 512, LANES), F32),
        *[pltpu.VMEM(c.shape, c.dtype) for c in consts],
        pltpu.VMEM((2, 2, WIDE, LANES), F32),
        pltpu.VMEM((2, 2, WIDE, LANES), F32),
        pltpu.VMEM((2, 2, LANES, WIDE), F32),
        slab(32),
        slab(32),
        wave,
        wave,
        wave,
        wave,
        wave,
        wave,
        slab(32),
        slab(32),
        slab(32),
        slab(32),
        pltpu.VMEM((2, 3, 2, LANES, WIDE), F32),
        pltpu.VMEM((2, 2, LANES, WIDE), F32),
        pltpu.VMEM((2, LANES, WIDE), F32),
        pltpu.VMEM((2 * SHARDS, 2, 8, LANES), F32),
        pltpu.VMEM((2 * SHARDS, 2, 8, LANES), F32),
        slab(8),
        slab(8),
        pltpu.VMEM((8, SHARDS, 8, LANES), F32),
        pltpu.VMEM((1024, LANES), F32),
        pltpu.SemaphoreType.DMA((9,)),
        pltpu.SemaphoreType.DMA((10,)),
        pltpu.SemaphoreType.DMA((10,)),
    ]
    anywhere = pl.BlockSpec(memory_space=pl.ANY)
    grad_input, grad_gate, grad_filter = pl.pallas_call(
        kernel,
        out_shape=[
            jax.ShapeDtypeStruct((SHARDS, 32, LANES), F32),
            jax.ShapeDtypeStruct((512, LANES), F32),
            jax.ShapeDtypeStruct((1024, LANES), F32),
        ],
        in_specs=[anywhere] * len(operands),
        out_specs=[anywhere] * 3,
        scratch_shapes=scratch,
        compiler_params=pltpu.CompilerParams(
            collective_id=0, has_side_effects=True, vmem_limit_bytes=40 * 2**20
        ),
        name="gated_conv_back",
    )(*operands)
    return (
        untiled(grad_input.reshape(512, LANES), 2),
        untiled(grad_gate, 2),
        untiled(grad_filter, 4),
    )


def solution(mesh):
    return jax.shard_map(
        per_device,
        mesh=mesh,
        in_specs=(
            P("ch", "ctx"),
            P("ch", "ctx"),
            P(None, "ch", "ctx", None),
            P(None, None, "ctx", None),
        ),
        out_specs=(P("ch", "ctx"), P("ch", "ctx"), P(None, "ctx")),
        check_vma=False,
    )
```

time: 471 us -> 86.6 us (0.18); the launches traced: 465 us -> 86.2 us
  other arithmetic: 165 us -> 0 us
  local copies, waits for them, and re-layouts: 113 us -> 12.1 us
  waiting for transfers between devices: 90.5 us -> 0 us
  Pallas kernels: 0 us -> 73.3 us
  matrix products: 40 us -> 0 us
  starting transfers between devices: 29.3 us -> 0 us
  blocking collectives: 25.6 us -> 0 us
    unnamed x1 -> x0, other arithmetic: 147 us -> none
    all_to_all x5 -> x0, waiting for transfers between devices: 90.5 us -> none  [the longest x1 47.9 us: from_everyone(): lax.all_to_all(jnp.broadcast_to(x[None], (devices, *x.shape)), axis, 0, 0...]
    pallas_call x0 -> x1, Pallas kernels: none -> 73.3 us  [per_device(): pl.pallas_call(kernel, out_shape=[jax.ShapeDtypeStruct((SHARDS, 32, LANES...]
    dot_general x20 -> x0, matrix products: 40 us -> none  [the longest x2 6.02 us: long_transform(): contract('...ca,ad->...dc', first_real, inner_sin)]
    unnamed x19 -> x21, local copies, waits for them, and re-layouts: 46.1 us -> 12.1 us
    reshape x7 -> x0, local copies, waits for them, and re-layouts: 33.6 us -> none  [the longest x1 23.9 us: per_device(): blocks = gated_grad.reshape(channels, time_rows, COLS)]
    all_to_all x5 -> x0, starting transfers between devices: 29.3 us -> none  [the longest x1 8.95 us: from_everyone(): lax.all_to_all(jnp.broadcast_to(x[None], (devices, *x.shape)), axis, 0, 0...]
    all_to_all x1 -> x0, blocking collectives: 25.6 us -> none  [exchange_in_pieces(): lax.all_to_all(slab, axis, split_axis=0, concat_axis=0, tiled=True)]
  transfers between devices with their start and end apart: 5 -> 0, of which waited for: 5 -> 0; matrix products, arithmetic and copies ran while one was open for 3% -> 0% of each run, Pallas kernels for 0% -> 0%
where the time goes in v1:
time: 86.6 us; the launch traced here: 86.2 us
  Pallas kernels  73.3 us (85%)
  local copies, waits for them, and re-layouts  12.1 us (14%)
    pallas_call x1, Pallas kernels, per_device(): pl.pallas_call(kernel, out_shape=[jax.ShapeDtypeStruct((SHARDS, 32, LANES...  73.3 us
    unnamed x21, local copies, waits for them, and re-layouts  12.1 us

profile of v1, /device:TPU:1, one launch (start us, length us, event | category | flops | bytes accessed | tf_op | source)
XLA Modules:
  0.0 86.2 jit_solution(7351531340595915759)
XLA Ops:
  0.6 0.0 copy-start
  0.6 1.6 %copy-done = f32[2,4,2,32768]{3,2,1,0:T(2,128)S(1)} copy-done((f32[2,4,2,32768]{3,2,1,0:T(2,128)S(1)}, f32[2,4,2,32768]{3,2,1,0:T(2,128)}, u32[]{:S(2)}) %copy-start) | copy-done | bytes 2097176
  2.2 0.0 copy-start.1
  2.2 1.6 %copy-done.1 = bf16[2,2,512,512]{3,2,1,0:T(8,128)(2,1)S(1)} copy-done((bf16[2,2,512,512]{3,2,1,0:T(8,128)(2,1)S(1)}, bf16[2,2,512,512]{3,2,1,0:T(8,128)(2,1)}, u32[]{:S(2)}) %copy-start.1) | copy-done | bytes 2097176
  3.8 0.0 copy-start.2
  3.8 1.2 %copy-done.2 = f32[2,2,2,32768]{3,2,1,0:T(2,128)S(1)} copy-done((f32[2,2,2,32768]{3,2,1,0:T(2,128)S(1)}, f32[2,2,2,32768]{3,2,1,0:T(2,128)}, u32[]{:S(2)}) %copy-start.2) | copy-done | bytes 1048600
  5.0 0.0 copy-start.3
  5.0 1.0 %copy-done.3 = bf16[2,2,256,256]{3,2,1,0:T(8,128)(2,1)S(1)} copy-done((bf16[2,2,256,256]{3,2,1,0:T(8,128)(2,1)S(1)}, bf16[2,2,256,256]{3,2,1,0:T(8,128)(2,1)}, u32[]{:S(2)}) %copy-start.3) | copy-done | bytes 524312
  6.1 0.0 copy-start.4
  6.1 0.9 %copy-done.4 = f32[2,32768]{1,0:T(2,128)S(1)} copy-done((f32[2,32768]{1,0:T(2,128)S(1)}, f32[2,32768]{1,0:T(2,128)}, u32[]{:S(2)}) %copy-start.4) | copy-done | bytes 262168
  7.0 0.0 copy-start.5
  7.0 0.9 %copy-done.5 = f32[2,32768]{1,0:T(2,128)S(1)} copy-done((f32[2,32768]{1,0:T(2,128)S(1)}, f32[2,32768]{1,0:T(2,128)}, u32[]{:S(2)}) %copy-start.5) | copy-done | bytes 262168
  8.0 0.0 copy-start.6
  8.0 0.9 %copy-done.6 = f32[2,256,128]{2,1,0:T(8,128)S(1)} copy-done((f32[2,256,128]{2,1,0:T(8,128)S(1)}, f32[2,256,128]{2,1,0:T(8,128)}, u32[]{:S(2)}) %copy-start.6) | copy-done | bytes 262168
  8.9 0.0 copy-start.7
  8.9 0.9 %copy-done.7 = f32[256,128]{1,0:T(8,128)S(1)} copy-done((f32[256,128]{1,0:T(8,128)S(1)}, f32[256,128]{1,0:T(8,128)}, u32[]{:S(2)}) %copy-start.7) | copy-done | bytes 131096
  9.8 0.0 copy-start.8
  9.8 0.8 copy-done.8
  10.6 73.3 %gated_conv_back.1 = (f32[16,32,128]{2,1,0:T(8,128)S(1)}, f32[512,128]{1,0:T(8,128)S(1)}, f32[1024,128]{1,0:T(8,128)S(1)}) custom-call(f32[512,128]{1,0:T(8,128)S(1)} %bitcast.38, f32[512,128]{1,0:T(8,128)S(1)} %bitcast.39, f32[2,2,512,128]{3,2,1,0:T(8,128)S(1)} %bitcast.36, f32[2,4,512,128]{3,2,1,0:T(8,128)S(1)} %bitcast.35, ...), custom_call_target="tpu_custom_call" | custom-call | tf_op jit(solution)/shard_map/gated_conv_back/pallas_call | solution.py:478
  84.0 0.7 copy.22
  84.7 0.7 copy.23
  85.4 0.8 copy.24
Async XLA Ops:
  0.6 1.6 %copy-start = (f32[2,4,2,32768]{3,2,1,0:T(2,128)S(1)}, f32[2,4,2,32768]{3,2,1,0:T(2,128)}, u32[]{:S(2)}) copy-start(f32[2,4,2,32768]{3,2,1,0:T(2,128)} %param.12) | copy-start | bytes 6291460
  2.2 1.6 %copy-start.1 = (bf16[2,2,512,512]{3,2,1,0:T(8,128)(2,1)S(1)}, bf16[2,2,512,512]{3,2,1,0:T(8,128)(2,1)}, u32[]{:S(2)}) copy-start(bf16[2,2,512,512]{3,2,1,0:T(8,128)(2,1)} %constant.10.clone.wide_hbm) | copy-start | bytes 6291460
  3.8 1.2 %copy-start.2 = (f32[2,2,2,32768]{3,2,1,0:T(2,128)S(1)}, f32[2,2,2,32768]{3,2,1,0:T(2,128)}, u32[]{:S(2)}) copy-start(f32[2,2,2,32768]{3,2,1,0:T(2,128)} %param.11) | copy-start | bytes 3145732
  5.0 1.0 %copy-start.3 = (bf16[2,2,256,256]{3,2,1,0:T(8,128)(2,1)S(1)}, bf16[2,2,256,256]{3,2,1,0:T(8,128)(2,1)}, u32[]{:S(2)}) copy-start(bf16[2,2,256,256]{3,2,1,0:T(8,128)(2,1)} %constant.11.clone.lanes_hbm) | copy-start | bytes 1572868
  6.1 0.9 %copy-start.4 = (f32[2,32768]{1,0:T(2,128)S(1)}, f32[2,32768]{1,0:T(2,128)}, u32[]{:S(2)}) copy-start(f32[2,32768]{1,0:T(2,128)} %param.9) | copy-start | bytes 786436
  7.0 0.9 %copy-start.5 = (f32[2,32768]{1,0:T(2,128)S(1)}, f32[2,32768]{1,0:T(2,128)}, u32[]{:S(2)}) copy-start(f32[2,32768]{1,0:T(2,128)} %param.10) | copy-start | bytes 786436
  8.0 0.9 %copy-start.6 = (f32[2,256,128]{2,1,0:T(8,128)S(1)}, f32[2,256,128]{2,1,0:T(8,128)}, u32[]{:S(2)}) copy-start(f32[2,256,128]{2,1,0:T(8,128)} %constant.12.clone.inner_hbm) | copy-start | bytes 786436
  8.9 0.9 %copy-start.7 = (f32[256,128]{1,0:T(8,128)S(1)}, f32[256,128]{1,0:T(8,128)}, u32[]{:S(2)}) copy-start(f32[256,128]{1,0:T(8,128)} %constant.14.clone.picked_hbm) | copy-start | bytes 393220
  9.8 0.8 copy-start.8

commit v2 on v1

--- a/solution.py
+++ b/solution.py
@@ -18,6 +18,10 @@
 WIDE = 256
 LANES = 128
 MESH = pl.DeviceIdType.MESH
+STEPS = (
+    (2, 2), (2, 1), (1, 2), (2, 3), (3, 2), (2, 0), (0, 2),
+    (1, 1), (3, 3), (1, 3), (3, 1), (1, 0), (0, 1), (3, 0), (0, 3),
+)
 F32 = jnp.float32
 BF16 = jnp.bfloat16
 
@@ -156,6 +160,7 @@
     core = group % 2
     plane = group // 2
     other = group + 1 - 2 * core
+    peers = [(me // 4 + dx) % 4 * 4 + (me + dz) % 4 for dx, dz in STEPS]
 
     def load(k, src, dst):
         copy = pltpu.make_async_copy(src, dst, load_sem.at[k])
@@ -176,8 +181,7 @@
 
     barrier = pltpu.get_barrier_semaphore()
     pl.semaphore_signal(barrier, inc=1, device_id={"ch": other}, device_id_type=MESH)
-    for step in range(1, SHARDS):
-        peer = (me + step) % SHARDS
+    for peer in peers:
         pl.semaphore_signal(barrier, inc=1, device_id={"ctx": peer}, device_id_type=MESH)
         pl.semaphore_signal(barrier, inc=1, device_id={"ctx": peer, "ch": other}, device_id_type=MESH)
     for step in range(1, 4):
@@ -187,8 +191,7 @@
     pl.semaphore_wait(barrier, 2 * SHARDS - 1 + 6)
 
     def send_all(k, out, into):
-        for step in range(1, SHARDS):
-            peer = (me + step) % SHARDS
+        for peer in peers:
             pltpu.make_async_remote_copy(
                 out.at[peer], into.at[me], send_sem.at[k], recv_sem.at[k],
                 device_id={"ctx": peer}, device_id_type=MESH,
@@ -332,10 +335,9 @@
     ((re, im),) = inverse_rows(core, [(fsum[core, 0] + fpart[0], fsum[core, 1] + fpart[1])])
     f_out[:, 0] = re.reshape(2 * SHARDS, 8, LANES)
     f_out[:, 1] = im.reshape(2 * SHARDS, 8, LANES)
-    for step in range(SHARDS):
-        peer = (me + step) % SHARDS
+    for peer in peers + [me]:
         for side in range(2):
-            if step == 0 and side == 0:
+            if peer is me and side == 0:
                 continue
             there = other if side else group
             half = 1 - core if side else core
@@ -474,7 +476,7 @@
         pltpu.SemaphoreType.DMA((10,)),
         pltpu.SemaphoreType.DMA((10,)),
     ]
-    anywhere = pl.BlockSpec(memory_space=pl.ANY)
+    anywhere = pl.BlockSpec(memory_space=pltpu.HBM)
     grad_input, grad_gate, grad_filter = pl.pallas_call(
         kernel,
         out_shape=[
@@ -486,7 +488,7 @@
         out_specs=[anywhere] * 3,
         scratch_shapes=scratch,
         compiler_params=pltpu.CompilerParams(
-            collective_id=0, has_side_effects=True, vmem_limit_bytes=40 * 2**20
+            collective_id=0, has_side_effects=True, vmem_limit_bytes=60 * 2**20
         ),
         name="gated_conv_back",
     )(*operands)

time: 86.6 us -> 77.8 us (0.90)
  the two profiles are of different devices: /device:TPU:1 before, /device:TPU:2 now
where the time goes in v2:
time: 77.8 us; the launch traced here: 77.6 us
  Pallas kernels  71.7 us (92%)
  local copies, waits for them, and re-layouts  5.21 us (7%)
    pallas_call x1, Pallas kernels, per_device(): pl.pallas_call(kernel, out_shape=[jax.ShapeDtypeStruct((SHARDS, 32, LANES...  71.7 us
    unnamed x3, local copies, waits for them, and re-layouts  5.21 us

profile of v2, /device:TPU:2, one launch (start us, length us, event | category | flops | bytes accessed | tf_op | source)
XLA Modules:
  0.0 77.6 jit_solution(15584770887804052770)
XLA Ops:
  0.6 71.7 %gated_conv_back.1 = (f32[16,32,128]{2,1,0:T(8,128)}, f32[512,128]{1,0:T(8,128)}, f32[1024,128]{1,0:T(8,128)}) custom-call(f32[512,128]{1,0:T(8,128)} %bitcast.38, f32[512,128]{1,0:T(8,128)} %bitcast.39, f32[2,2,512,128]{3,2,1,0:T(8,128)} %bitcast.36, f32[2,4,512,128]{3,2,1,0:T(8,128)} %bitcast.35, bf16[2,2,512,512]{3,2,1,0:T(8,128)(2,1)} %constant.10.clone.wide_hbm, ...), custom_call_target="tpu_custom_call" | custom-call | tf_op jit(solution)/shard_map/gated_conv_back/pallas_call | solution.py:480
  72.4 1.7 %copy.22 = f32[2,32768]{1,0:T(2,128)} copy(f32[2,32768]{1,0:T(2,128)} %bitcast.41) | data formatting | bytes 524288
  74.1 1.7 %copy.23 = f32[2,32768]{1,0:T(2,128)} copy(f32[2,32768]{1,0:T(2,128)} %bitcast.40) | data formatting | bytes 524288
  75.7 1.9 %copy.24 = f32[4,32768]{1,0:T(4,128)} copy(f32[4,32768]{1,0:T(4,128)} %bitcast.37) | data formatting | bytes 1048576

commit v3 on v2

--- a/solution.py
+++ b/solution.py
@@ -148,7 +148,7 @@
 
 def kernel(
     grad_hbm, gate_hbm, spec_hbm, filt_hbm, wide_hbm, lanes_hbm, inner_hbm, lane_rows_hbm, picked_hbm,
-    gi_hbm, gg_hbm, gf_hbm,
+    gi_out, gg_out, gf_out,
     grad, gate, spec, filt, wide, lanes, inner, lane_rows, picked,
     pre, mid, midt,
     x_out, x_in, y_out, y_in, c_out, c_in, i_out, i_in, d_out, d_in, e_out, e_in,
@@ -173,14 +173,13 @@
         load(2, inner_hbm, inner),
         load(3, lane_rows_hbm, lane_rows),
         load(4, picked_hbm, picked),
-        load(5, spec_hbm, spec),
-        load(6, filt_hbm.at[:, plane], filt),
+        load(5, filt_hbm.at[:, plane], filt),
+        load(6, spec_hbm, spec),
         load(7, lanes_hbm, lanes),
         load(8, wide_hbm, wide),
     ]
 
     barrier = pltpu.get_barrier_semaphore()
-    pl.semaphore_signal(barrier, inc=1, device_id={"ch": other}, device_id_type=MESH)
     for peer in peers:
         pl.semaphore_signal(barrier, inc=1, device_id={"ctx": peer}, device_id_type=MESH)
         pl.semaphore_signal(barrier, inc=1, device_id={"ctx": peer, "ch": other}, device_id_type=MESH)
@@ -188,7 +187,7 @@
         for side in range(2):
             there = 2 * ((plane + step) % 4) + side
             pl.semaphore_signal(barrier, inc=1, device_id={"ch": there}, device_id_type=MESH)
-    pl.semaphore_wait(barrier, 2 * SHARDS - 1 + 6)
+    pl.semaphore_signal(barrier, inc=1, device_id={"ch": other}, device_id_type=MESH)
 
     def send_all(k, out, into):
         for peer in peers:
@@ -212,7 +211,6 @@
     loads[0].wait()
     loads[1].wait()
     x_out[...] = (grad[...] * gate[...]).reshape(SHARDS, 32, LANES)
-    send_all(0, x_out, x_in)
 
     for k in (2, 3, 4):
         loads[k].wait()
@@ -231,11 +229,17 @@
         midt[b, 0] = tr.T * 0.5
         midt[b, 1] = ti.T * 0.5
 
-    for k in (5, 6, 7, 8):
-        loads[k].wait()
-
     def spread(ref, b):
         return jnp.concatenate([ref[pl.ds(2 * s + b, LANES, stride=4), :] for s in range(2)], axis=1)
+
+    loads[5].wait()
+    loads[6].wait()
+    for b in range(2):
+        prods[b, 0, 0], prods[b, 0, 1] = spread(filt.at[0], b), spread(filt.at[1], b)
+        for ch in range(2):
+            prods[b, 1 + ch, 0], prods[b, 1 + ch, 1] = spread(spec.at[0, ch], b), spread(spec.at[1, ch], b)
+    loads[7].wait()
+    loads[8].wait()
 
     def inverse_rows(b, arrays):
         mr, mi = midt[b, 0], midt[b, 1]
@@ -253,28 +257,19 @@
             out.append((sr * pr + si * pi, si * pr - sr * pi))
         return out
 
-    def fill(out, b, arrays):
-        for ch, (re, im) in enumerate(inverse_rows(b, arrays)):
-            out[:, b, 0, ch] = re.reshape(SHARDS, 16, LANES)
-            out[:, b, 1, ch] = im.reshape(SHARDS, 16, LANES)
-
-    for b in range(2):
-        hr, hi = spread(filt.at[0], b), spread(filt.at[1], b)
-        prods[b, 0, 0], prods[b, 0, 1] = hr, hi
-        for ch in range(2):
-            ur, ui = spread(spec.at[0, ch], b), spread(spec.at[1, ch], b)
-            prods[b, 1 + ch, 0], prods[b, 1 + ch, 1] = ur, ui
-
-    def conv_row(b, carry):
+    pl.semaphore_wait(barrier, 2 * SHARDS - 1 + 6)
+
+    send_all(0, x_out, x_in)
+
+    def conv_row(b):
         hr, hi = prods[b, 0, 0], prods[b, 0, 1]
         arrays = []
         for ch in range(2):
             ur, ui = prods[b, 1 + ch, 0], prods[b, 1 + ch, 1]
             arrays.append((ur * hr - ui * hi, ur * hi + ui * hr))
-        fill(c_out, b, arrays)
-        return carry
-
-    arrived(0, x_in)
+        for ch, (re, im) in enumerate(inverse_rows(b, arrays)):
+            c_out[b, :, 0, ch] = re.reshape(SHARDS, 16, LANES)
+            c_out[b, :, 1, ch] = im.reshape(SHARDS, 16, LANES)
 
     def slab_forward(step, carry):
         ch, half = step // 2, step % 2
@@ -287,23 +282,38 @@
                 im = jnp.zeros_like(re)
             elif r > RADIX // 2:
                 im = -im
-            y_out[r // 2, r % 2, 0, ch, at, :] = re
-            y_out[r // 2, r % 2, 1, ch, at, :] = im
+            y_out[r % 2, r // 2, 0, ch, at, :] = re
+            y_out[r % 2, r // 2, 1, ch, at, :] = im
         return carry
 
-    lax.fori_loop(0, 4, slab_forward, 0)
-    send_all(1, y_out, y_in)
-
-    lax.fori_loop(0, 2, conv_row, 0)
-    send_all(2, c_out, c_in)
-
-    arrived(1, y_in)
-
-    def forward_row(b, carry):
+    def conv_step(step, carry):
+        conv_row(step)
+
+        @pl.when(step == 0)
+        def _():
+            send_all(3, c_out.at[0], c_in.at[0])
+            arrived(0, x_in)
+            lax.fori_loop(0, 4, slab_forward, 0)
+            for turn in range(2):
+                b = (1 - core + turn) % 2
+                send_all(1 + turn, y_out.at[b], y_in.at[b])
+
+        return carry
+
+    lax.fori_loop(0, 2, conv_step, 0)
+    send_all(4, c_out.at[1], c_in.at[1])
+
+    swap = pltpu.make_async_remote_copy(
+        fsum.at[1 - core], fpart, send_sem.at[5], recv_sem.at[5], device_id={"ch": other}, device_id_type=MESH
+    )
+
+    def forward_row(turn, carry):
+        b = (1 - core + turn) % 2
+        bulk(1 + turn, y_in.at[b, pl.ds(0, SHARDS - 1)]).wait_recv()
         pr = jnp.concatenate([pre[b, 0]] * 2, axis=1)
         pi = jnp.concatenate([pre[b, 1]] * 2, axis=1)
-        yr = jnp.concatenate([y_in[:, b, 0, ch].reshape(WIDE, LANES) for ch in range(2)], axis=1)
-        yi = jnp.concatenate([y_in[:, b, 1, ch].reshape(WIDE, LANES) for ch in range(2)], axis=1)
+        yr = jnp.concatenate([y_in[b, :, 0, ch].reshape(WIDE, LANES) for ch in range(2)], axis=1)
+        yi = jnp.concatenate([y_in[b, :, 1, ch].reshape(WIDE, LANES) for ch in range(2)], axis=1)
         a = product(wide[0], jnp.concatenate([yr * pr - yi * pi, yr * pi + yi * pr], axis=0))
         mr, mi = mid[b, 0], mid[b, 1]
         fr = fi = None
@@ -318,19 +328,14 @@
             hr, hi = prods[b, 0, 0], prods[b, 0, 1]
             prods[b, 1 + ch, 0], prods[b, 1 + ch, 1] = hr * gr + hi * gi, hr * gi - hi * gr
         fsum[b, 0], fsum[b, 1] = fr, fi
+
+        @pl.when(turn == 0)
+        def _():
+            swap.start()
+
         return carry
 
     lax.fori_loop(0, 2, forward_row, 0)
-
-    swap = pltpu.make_async_remote_copy(
-        fsum.at[1 - core], fpart, send_sem.at[3], recv_sem.at[3], device_id={"ch": other}, device_id_type=MESH
-    )
-    swap.start()
-
-    def input_row(b, carry):
-        fill(i_out, b, [(prods[b, 1 + ch, 0], prods[b, 1 + ch, 1]) for ch in range(2)])
-        return carry
-
     swap.wait_recv()
     ((re, im),) = inverse_rows(core, [(fsum[core, 0] + fpart[0], fsum[core, 1] + fpart[1])])
     f_out[:, 0] = re.reshape(2 * SHARDS, 8, LANES)
@@ -342,91 +347,129 @@
             there = other if side else group
             half = 1 - core if side else core
             pltpu.make_async_remote_copy(
-                f_out.at[2 * peer + half], f_in.at[2 * me + core], send_sem.at[4], recv_sem.at[4],
+                f_out.at[2 * peer + half], f_in.at[2 * me + core], send_sem.at[6], recv_sem.at[6],
                 device_id={"ctx": peer, "ch": there}, device_id_type=MESH,
             ).start()
     f_in[2 * me + core] = f_out[2 * me + core]
 
+    def input_row(b, carry):
+        arrays = [(prods[b, 1 + ch, 0], prods[b, 1 + ch, 1]) for ch in range(2)]
+        for ch, both in enumerate(inverse_rows(b, arrays)):
+            for ri in range(2):
+                pieces = both[ri].reshape(SHARDS, 16, LANES)
+                for half in range(2):
+                    i_out[half, :, b, ri, ch] = pieces[:, 8 * half : 8 * half + 8]
+        return carry
+
     lax.fori_loop(0, 2, input_row, 0)
-    send_all(5, i_out, i_in)
-
-    def slab_back(src, out):
-        def body(half, carry):
-            at = pl.ds(pl.multiple_of(8 * half, 8), 8)
-
-            def row(r, ri, ch):
-                return src[r // 2, r % 2, ri, ch, at, :]
-
-            ws = [None] * RADIX
-            for r in range(RADIX // 2 + 1):
-                q = (RADIX - r) % RADIX
-                a = row(r, 0, 0) + row(q, 0, 0)
-                c = row(r, 0, 1) + row(q, 0, 1)
-                if q == r:
-                    ws[r] = (a, c)
-                    continue
-                bb = row(r, 1, 0) - row(q, 1, 0)
-                d = row(r, 1, 1) - row(q, 1, 1)
-                ws[r] = (a - d, bb + c)
-                ws[q] = (a + d, c - bb)
-            for j, (re, im) in enumerate(back_dft(ws, first_half=True)):
-                out[j, pl.ds(16 * half, 8, stride=2), :] = re
-                out[j, pl.ds(16 * half + 1, 8, stride=2), :] = im
-            return carry
-
-        lax.fori_loop(0, 2, body, 0)
-
-    arrived(2, c_in)
-    slab_back(c_in, d_out)
-    send_all(6, d_out, d_in)
-
-    bulk(4, f_in.at[pl.ds(0, 2 * SHARDS - 1)]).wait_recv()
+    send_all(7, i_out.at[0], i_in.at[0])
+
+    bulk(6, f_in.at[pl.ds(0, 2 * SHARDS - 1)]).wait_recv()
     ws = [(f_in[r, 0], f_in[r, 1]) for r in range(RADIX)]
     for j, (re, _) in enumerate(back_dft(ws, first_half=True)):
         g_out[j] = re + re
-    send_all(7, g_out, g_in)
-
-    arrived(5, i_in)
-    slab_back(i_in, e_out)
-    send_all(8, e_out, e_in)
-
-    arrived(7, g_in)
-    for step in range(4):
-        for side in range(2):
-            if step == 0 and side == 0:
+    send_all(10, g_out, g_in)
+    send_all(8, i_out.at[1], i_in.at[1])
+
+    def slab_back(row, put):
+        ws = [None] * RADIX
+        for r in range(RADIX // 2 + 1):
+            q = (RADIX - r) % RADIX
+            a = row(r, 0, 0) + row(q, 0, 0)
+            c = row(r, 0, 1) + row(q, 0, 1)
+            if q == r:
+                ws[r] = (a, c)
                 continue
-            there = 2 * ((plane + step) % 4) + (1 - core if side else core)
+            bb = row(r, 1, 0) - row(q, 1, 0)
+            d = row(r, 1, 1) - row(q, 1, 1)
+            ws[r] = (a - d, bb + c)
+            ws[q] = (a + d, c - bb)
+        for j, (re, im) in enumerate(back_dft(ws, first_half=True)):
+            put(j, 0, re)
+            put(j, 1, im)
+
+    def conv_back(half, carry):
+        at = pl.ds(pl.multiple_of(8 * half, 8), 8)
+
+        def put(j, ch, value):
+            d_out[j, pl.ds(16 * half + ch, 8, stride=2), :] = value
+
+        slab_back(lambda r, ri, ch: c_in[r % 2, r // 2, ri, ch, at, :], put)
+        return carry
+
+    arrived(3, c_in.at[0])
+    arrived(4, c_in.at[1])
+    lax.fori_loop(0, 2, conv_back, 0)
+    send_all(9, d_out, d_in)
+
+    def input_back(half, carry):
+        bulk(7 + half, i_in.at[half, pl.ds(0, SHARDS - 1)]).wait_recv()
+
+        def put(j, ch, value):
+            e_out[half, j, pl.ds(ch, 8, stride=2), :] = value
+
+        slab_back(lambda r, ri, ch: i_in[half, r // 2, r % 2, ri, ch], put)
+        for peer in peers:
             pltpu.make_async_remote_copy(
-                g_in, g_all.at[group], send_sem.at[9], recv_sem.at[9],
-                device_id={"ch": there}, device_id_type=MESH,
+                e_out.at[half, peer], e_in.at[me, half], send_sem.at[11 + half], recv_sem.at[11 + half],
+                device_id={"ctx": peer}, device_id_type=MESH,
             ).start()
-    g_all[group] = g_in[...]
-
-    arrived(6, d_in)
+        e_in[me, half] = e_out[half, me]
+
+        @pl.when(half == 0)
+        def _():
+            arrived(10, g_in)
+            for step in range(4):
+                for side in range(2):
+                    if step == 0 and side == 0:
+                        continue
+                    there = 2 * ((plane + step) % 4) + (1 - core if side else core)
+                    pltpu.make_async_remote_copy(
+                        g_in, g_all.at[group], send_sem.at[13], recv_sem.at[13],
+                        device_id={"ch": there}, device_id_type=MESH,
+                    ).start()
+            g_all[group] = g_in[...]
+
+        return carry
+
+    lax.fori_loop(0, 2, input_back, 0)
+
+    arrived(9, d_in)
     gate[...] = grad[...] * d_in[...].reshape(512, LANES)
-    store_gg = load(1, gate, gg_hbm)
-    arrived(8, e_in)
-    store_gi = load(0, e_in, gi_hbm)
-    bulk(9, g_all.at[pl.ds(0, 7)]).wait_recv()
+    store_gg = load(1, gate, gg_out)
+    bulk(13, g_all.at[pl.ds(0, 7)]).wait_recv()
     for f in range(FILTERS):
         for c in range(2):
             for q in range(SHARDS):
                 gf[pl.ds(64 * q + 32 * c + f, 8, stride=4), :] = g_all[2 * f + c, q]
-    store_gf = load(2, gf, gf_hbm)
+    store_gf = load(2, gf, gf_out)
+    bulk(11, e_out.at[0, pl.ds(0, SHARDS - 1)]).wait_recv()
+    bulk(12, e_out.at[1, pl.ds(0, SHARDS - 1)]).wait_recv()
+    store_gi = load(0, e_in, gi_out)
 
     left(0, x_out)
-    left(1, y_out)
-    left(2, c_out)
+    for turn in range(2):
+        left(1 + turn, y_out.at[turn])
+        left(3 + turn, c_out.at[turn])
+        left(7 + turn, i_out.at[turn])
+        left(11 + turn, e_out.at[turn])
     swap.wait_send()
-    bulk(4, f_out.at[pl.ds(0, 2 * SHARDS - 1)]).wait_send()
-    left(5, i_out)
-    left(6, d_out)
-    left(7, g_out)
-    left(8, e_out)
-    bulk(9, g_all.at[pl.ds(0, 7)]).wait_send()
+    bulk(6, f_out.at[pl.ds(0, 2 * SHARDS - 1)]).wait_send()
+    left(9, d_out)
+    left(10, g_out)
+    bulk(13, g_all.at[pl.ds(0, 7)]).wait_send()
     store_gg.wait()
+    store_gf.wait()
     store_gi.wait()
-    store_gf.wait()
+
+
+def store_results(*refs):
+    ins, outs, sem = refs[:3], refs[3:6], refs[6]
+    copies = [pltpu.make_async_copy(src, dst, sem.at[k]) for k, (src, dst) in enumerate(zip(ins, outs))]
+    for copy in copies:
+        copy.start()
+    for copy in copies:
+        copy.wait()
 
 
 def per_device(grad_out, gate_in, input_spectrum, filter_spectrum):
@@ -441,7 +484,8 @@
     consts = tables()
     operands = (tiled(grad_out), tiled(gate_in), tiled(input_spectrum), tiled(filter_spectrum), *consts)
     slab = lambda *dims: pltpu.VMEM((SHARDS, *dims, LANES), F32)
-    wave = slab(2, 2, 2, 16)
+    wave = pltpu.VMEM((2, SHARDS, 2, 2, 16, LANES), F32)
+    half_wave = pltpu.VMEM((2, SHARDS, 2, 2, 2, 8, LANES), F32)
     scratch = [
         pltpu.VMEM((512, LANES), F32),
         pltpu.VMEM((512, LANES), F32),
@@ -457,12 +501,12 @@
         wave,
         wave,
         wave,
-        wave,
-        wave,
+        half_wave,
+        half_wave,
         slab(32),
         slab(32),
-        slab(32),
-        slab(32),
+        pltpu.VMEM((2, SHARDS, 16, LANES), F32),
+        pltpu.VMEM((SHARDS, 2, 16, LANES), F32),
         pltpu.VMEM((2, 3, 2, LANES, WIDE), F32),
         pltpu.VMEM((2, 2, LANES, WIDE), F32),
         pltpu.VMEM((2, LANES, WIDE), F32),
@@ -473,25 +517,36 @@
         pltpu.VMEM((8, SHARDS, 8, LANES), F32),
         pltpu.VMEM((1024, LANES), F32),
         pltpu.SemaphoreType.DMA((9,)),
-        pltpu.SemaphoreType.DMA((10,)),
-        pltpu.SemaphoreType.DMA((10,)),
+        pltpu.SemaphoreType.DMA((14,)),
+        pltpu.SemaphoreType.DMA((14,)),
     ]
-    anywhere = pl.BlockSpec(memory_space=pltpu.HBM)
-    grad_input, grad_gate, grad_filter = pl.pallas_call(
+    in_hbm = pl.BlockSpec(memory_space=pltpu.HBM)
+    anywhere = pl.BlockSpec(memory_space=pl.ANY)
+    results = [
+        jax.ShapeDtypeStruct((SHARDS, 2, 16, LANES), F32),
+        jax.ShapeDtypeStruct((512, LANES), F32),
+        jax.ShapeDtypeStruct((1024, LANES), F32),
+    ]
+    found = pl.pallas_call(
         kernel,
-        out_shape=[
-            jax.ShapeDtypeStruct((SHARDS, 32, LANES), F32),
-            jax.ShapeDtypeStruct((512, LANES), F32),
-            jax.ShapeDtypeStruct((1024, LANES), F32),
-        ],
-        in_specs=[anywhere] * len(operands),
+        out_shape=results,
+        in_specs=[in_hbm] * len(operands),
         out_specs=[anywhere] * 3,
         scratch_shapes=scratch,
         compiler_params=pltpu.CompilerParams(
-            collective_id=0, has_side_effects=True, vmem_limit_bytes=60 * 2**20
+            collective_id=0, has_side_effects=True, vmem_limit_bytes=40 * 2**20
         ),
         name="gated_conv_back",
-    )(*operands)
+    )(*[pltpu.with_memory_space_constraint(x, pltpu.HBM) for x in operands])
+    grad_input, grad_gate, grad_filter = pl.pallas_call(
+        store_results,
+        out_shape=results,
+        in_specs=[anywhere] * 3,
+        out_specs=[in_hbm] * 3,
+        scratch_shapes=[pltpu.SemaphoreType.DMA((3,))],
+        compiler_params=pltpu.CompilerParams(vmem_limit_bytes=2**20),
+        name="store_results",
+    )(*found)
     return (
         untiled(grad_input.reshape(512, LANES), 2),
         untiled(grad_gate, 2),

time: 77.8 us -> 59.4 us (0.76)
  the two profiles are of different devices: /device:TPU:2 before, /device:TPU:1 now
where the time goes in v3:
time: 59.4 us; the launch traced here: 59.3 us
  Pallas kernels  58.6 us (99%)
  between operations  0.64 us (1%)
    pallas_call x1, Pallas kernels, per_device(): pl.pallas_call(kernel, out_shape=results, in_specs=[in_hbm] * len(operand...  57.6 us

profile of v3, /device:TPU:1, one launch (start us, length us, event | category | flops | bytes accessed | tf_op | source)
XLA Modules:
  0.0 59.3 jit_solution(8189584348569927834)
XLA Ops:
  0.6 57.6 %gated_conv_back.1 = (f32[16,2,16,128]{3,2,1,0:T(8,128)S(1)}, f32[512,128]{1,0:T(8,128)S(1)}, f32[1024,128]{1,0:T(8,128)S(1)}) custom-call(f32[512,128]{1,0:T(8,128)} %bitcast.37, f32[512,128]{1,0:T(8,128)} %bitcast.38, f32[2,2,512,128]{3,2,1,0:T(8,128)} %bitcast.36, f32[2,4,512,128]{3,2,1,0:T(8,128)} %bitcast.35, ...), custom_call_target="tpu_custom_call" | custom-call | tf_op jit(solution)/shard_map/gated_conv_back/pallas_call | solution.py:530
  58.3 1.0 %store_results.1 = (f32[16,2,16,128]{3,2,1,0:T(8,128)}, f32[512,128]{1,0:T(8,128)}, f32[1024,128]{1,0:T(8,128)}) custom-call(f32[16,2,16,128]{3,2,1,0:T(8,128)S(1)} %get-tuple-element.9.refs_0_, f32[512,128]{1,0:T(8,128)S(1)} %get-tuple-element.10.refs_1_, f32[1024,128]{1,0:T(8,128)S(1)} %get-tuple-element.11.refs_2_), custom_call_target="tpu_custom_call" | custom-call | tf_op jit(solution)/shard_map/store_results/pallas_call | solution.py:541

commit v4 on v3

--- a/solution.py
+++ b/solution.py
@@ -151,7 +151,7 @@
     gi_out, gg_out, gf_out,
     grad, gate, spec, filt, wide, lanes, inner, lane_rows, picked,
     pre, mid, midt,
-    x_out, x_in, y_out, y_in, c_out, c_in, i_out, i_in, d_out, d_in, e_out, e_in,
+    x_out, x_in, y_out, y_in, c_out, c_in, i_out, i_in, d_out, d_in, e_out,
     prods, fsum, fpart, f_out, f_in, g_out, g_in, g_all, gf,
     load_sem, send_sem, recv_sem,
 ):
@@ -161,6 +161,16 @@
     plane = group // 2
     other = group + 1 - 2 * core
     peers = [(me // 4 + dx) % 4 * 4 + (me + dz) % 4 for dx, dz in STEPS]
+
+    barrier = pltpu.get_barrier_semaphore()
+    for peer in peers:
+        pl.semaphore_signal(barrier, inc=1, device_id={"ctx": peer}, device_id_type=MESH)
+        pl.semaphore_signal(barrier, inc=1, device_id={"ctx": peer, "ch": other}, device_id_type=MESH)
+    for step in range(1, 4):
+        for side in range(2):
+            there = 2 * ((plane + step) % 4) + side
+            pl.semaphore_signal(barrier, inc=1, device_id={"ch": there}, device_id_type=MESH)
+    pl.semaphore_signal(barrier, inc=1, device_id={"ch": other}, device_id_type=MESH)
 
     def load(k, src, dst):
         copy = pltpu.make_async_copy(src, dst, load_sem.at[k])
@@ -178,16 +188,6 @@
         load(7, lanes_hbm, lanes),
         load(8, wide_hbm, wide),
     ]
-
-    barrier = pltpu.get_barrier_semaphore()
-    for peer in peers:
-        pl.semaphore_signal(barrier, inc=1, device_id={"ctx": peer}, device_id_type=MESH)
-        pl.semaphore_signal(barrier, inc=1, device_id={"ctx": peer, "ch": other}, device_id_type=MESH)
-    for step in range(1, 4):
-        for side in range(2):
-            there = 2 * ((plane + step) % 4) + side
-            pl.semaphore_signal(barrier, inc=1, device_id={"ch": there}, device_id_type=MESH)
-    pl.semaphore_signal(barrier, inc=1, device_id={"ch": other}, device_id_type=MESH)
 
     def send_all(k, out, into):
         for peer in peers:
@@ -307,7 +307,7 @@
         fsum.at[1 - core], fpart, send_sem.at[5], recv_sem.at[5], device_id={"ch": other}, device_id_type=MESH
     )
 
-    def forward_row(turn, carry):
+    def forward_row(turn):
         b = (1 - core + turn) % 2
         bulk(1 + turn, y_in.at[b, pl.ds(0, SHARDS - 1)]).wait_recv()
         pr = jnp.concatenate([pre[b, 0]] * 2, axis=1)
@@ -329,47 +329,59 @@
             prods[b, 1 + ch, 0], prods[b, 1 + ch, 1] = hr * gr + hi * gi, hr * gi - hi * gr
         fsum[b, 0], fsum[b, 1] = fr, fi
 
-        @pl.when(turn == 0)
-        def _():
-            swap.start()
-
-        return carry
-
-    lax.fori_loop(0, 2, forward_row, 0)
-    swap.wait_recv()
-    ((re, im),) = inverse_rows(core, [(fsum[core, 0] + fpart[0], fsum[core, 1] + fpart[1])])
-    f_out[:, 0] = re.reshape(2 * SHARDS, 8, LANES)
-    f_out[:, 1] = im.reshape(2 * SHARDS, 8, LANES)
-    for peer in peers + [me]:
-        for side in range(2):
-            if peer is me and side == 0:
-                continue
-            there = other if side else group
-            half = 1 - core if side else core
-            pltpu.make_async_remote_copy(
-                f_out.at[2 * peer + half], f_in.at[2 * me + core], send_sem.at[6], recv_sem.at[6],
-                device_id={"ctx": peer, "ch": there}, device_id_type=MESH,
-            ).start()
-    f_in[2 * me + core] = f_out[2 * me + core]
-
-    def input_row(b, carry):
+        return b
+
+    def input_row(b):
         arrays = [(prods[b, 1 + ch, 0], prods[b, 1 + ch, 1]) for ch in range(2)]
         for ch, both in enumerate(inverse_rows(b, arrays)):
             for ri in range(2):
                 pieces = both[ri].reshape(SHARDS, 16, LANES)
                 for half in range(2):
-                    i_out[half, :, b, ri, ch] = pieces[:, 8 * half : 8 * half + 8]
+                    i_out[b, :, half, ri, ch] = pieces[:, 8 * half : 8 * half + 8]
+
+    def filter_row():
+        swap.wait_recv()
+        ((re, im),) = inverse_rows(core, [(fsum[core, 0] + fpart[0], fsum[core, 1] + fpart[1])])
+        f_out[:, 0] = re.reshape(2 * SHARDS, 8, LANES)
+        f_out[:, 1] = im.reshape(2 * SHARDS, 8, LANES)
+        for peer in peers + [me]:
+            for side in range(2):
+                if peer is me and side == 0:
+                    continue
+                there = other if side else group
+                half = 1 - core if side else core
+                pltpu.make_async_remote_copy(
+                    f_out.at[2 * peer + half], f_in.at[2 * me + core], send_sem.at[6], recv_sem.at[6],
+                    device_id={"ctx": peer, "ch": there}, device_id_type=MESH,
+                ).start()
+        f_in[2 * me + core] = f_out[2 * me + core]
+
+    def row_turn(turn, carry):
+        b = forward_row(turn)
+
+        @pl.when(turn == 0)
+        def _():
+            swap.start()
+
+        @pl.when(turn == 1)
+        def _():
+            filter_row()
+
+        input_row(b)
+
+        @pl.when(turn == 0)
+        def _():
+            send_all(7, i_out.at[1 - core], i_in.at[1 - core])
+
         return carry
 
-    lax.fori_loop(0, 2, input_row, 0)
-    send_all(7, i_out.at[0], i_in.at[0])
-
-    bulk(6, f_in.at[pl.ds(0, 2 * SHARDS - 1)]).wait_recv()
-    ws = [(f_in[r, 0], f_in[r, 1]) for r in range(RADIX)]
-    for j, (re, _) in enumerate(back_dft(ws, first_half=True)):
-        g_out[j] = re + re
-    send_all(10, g_out, g_in)
-    send_all(8, i_out.at[1], i_in.at[1])
+    lax.fori_loop(0, 2, row_turn, 0)
+    for peer in peers:
+        pltpu.make_async_remote_copy(
+            i_out.at[core, peer, 0], i_in.at[core, me, 0], send_sem.at[8], recv_sem.at[8],
+            device_id={"ctx": peer}, device_id_type=MESH,
+        ).start()
+    i_in[core, me] = i_out[core, me]
 
     def slab_back(row, put):
         ws = [None] * RADIX
@@ -402,65 +414,89 @@
     lax.fori_loop(0, 2, conv_back, 0)
     send_all(9, d_out, d_in)
 
+    bulk(6, f_in.at[pl.ds(0, 2 * SHARDS - 1)]).wait_recv()
+    ws = [(f_in[r, 0], f_in[r, 1]) for r in range(RADIX)]
+    for j, (re, _) in enumerate(back_dft(ws, first_half=True)):
+        g_out[j] = re + re
+    send_all(10, g_out, g_in)
+    for peer in peers:
+        pltpu.make_async_remote_copy(
+            i_out.at[core, peer, 1], i_in.at[core, me, 1], send_sem.at[15], recv_sem.at[15],
+            device_id={"ctx": peer}, device_id_type=MESH,
+        ).start()
+
+    arrived(7, i_in.at[1 - core])
+
+    def half_of(ref, half):
+        return ref.at[core, pl.ds(0, SHARDS - 1), half]
+
+    share = pltpu.make_async_remote_copy(
+        g_all.at[core], g_all.at[core], send_sem.at[14], recv_sem.at[14],
+        device_id={"ch": other}, device_id_type=MESH,
+    )
+
     def input_back(half, carry):
-        bulk(7 + half, i_in.at[half, pl.ds(0, SHARDS - 1)]).wait_recv()
+        bulk(8 + 7 * half, half_of(i_in, half)).wait_recv()
 
         def put(j, ch, value):
             e_out[half, j, pl.ds(ch, 8, stride=2), :] = value
 
-        slab_back(lambda r, ri, ch: i_in[half, r // 2, r % 2, ri, ch], put)
+        slab_back(lambda r, ri, ch: i_in[r % 2, r // 2, half, ri, ch], put)
         for peer in peers:
             pltpu.make_async_remote_copy(
-                e_out.at[half, peer], e_in.at[me, half], send_sem.at[11 + half], recv_sem.at[11 + half],
+                e_out.at[half, peer], gi_out.at[me, half], send_sem.at[11 + half], recv_sem.at[11 + half],
                 device_id={"ctx": peer}, device_id_type=MESH,
             ).start()
-        e_in[me, half] = e_out[half, me]
+        own = pltpu.make_async_copy(e_out.at[half, me], gi_out.at[me, half], load_sem.at[half])
+        own.start()
 
         @pl.when(half == 0)
         def _():
             arrived(10, g_in)
-            for step in range(4):
-                for side in range(2):
-                    if step == 0 and side == 0:
-                        continue
-                    there = 2 * ((plane + step) % 4) + (1 - core if side else core)
-                    pltpu.make_async_remote_copy(
-                        g_in, g_all.at[group], send_sem.at[13], recv_sem.at[13],
-                        device_id={"ch": there}, device_id_type=MESH,
-                    ).start()
-            g_all[group] = g_in[...]
-
+            for step in range(1, 4):
+                pltpu.make_async_remote_copy(
+                    g_in, g_all.at[core, plane], send_sem.at[13], recv_sem.at[13],
+                    device_id={"ch": 2 * ((plane + step) % 4) + core}, device_id_type=MESH,
+                ).start()
+            g_all[core, plane] = g_in[...]
+
+        @pl.when(half == 1)
+        def _():
+            bulk(13, g_all.at[core, pl.ds(0, 3)]).wait_recv()
+            share.start()
+
+        own.wait()
         return carry
 
     lax.fori_loop(0, 2, input_back, 0)
 
     arrived(9, d_in)
     gate[...] = grad[...] * d_in[...].reshape(512, LANES)
-    store_gg = load(1, gate, gg_out)
-    bulk(13, g_all.at[pl.ds(0, 7)]).wait_recv()
+    store_gg = load(2, gate, gg_out)
+    share.wait_recv()
     for f in range(FILTERS):
         for c in range(2):
             for q in range(SHARDS):
-                gf[pl.ds(64 * q + 32 * c + f, 8, stride=4), :] = g_all[2 * f + c, q]
-    store_gf = load(2, gf, gf_out)
+                gf[pl.ds(64 * q + 32 * c + f, 8, stride=4), :] = g_all[c, f, q]
+    store_gf = load(3, gf, gf_out)
     bulk(11, e_out.at[0, pl.ds(0, SHARDS - 1)]).wait_recv()
     bulk(12, e_out.at[1, pl.ds(0, SHARDS - 1)]).wait_recv()
-    store_gi = load(0, e_in, gi_out)
 
     left(0, x_out)
     for turn in range(2):
         left(1 + turn, y_out.at[turn])
         left(3 + turn, c_out.at[turn])
-        left(7 + turn, i_out.at[turn])
+        bulk(8 + 7 * turn, half_of(i_out, turn)).wait_send()
         left(11 + turn, e_out.at[turn])
     swap.wait_send()
     bulk(6, f_out.at[pl.ds(0, 2 * SHARDS - 1)]).wait_send()
+    left(7, i_out.at[1 - core])
     left(9, d_out)
     left(10, g_out)
-    bulk(13, g_all.at[pl.ds(0, 7)]).wait_send()
+    bulk(13, g_all.at[core, pl.ds(0, 3)]).wait_send()
+    share.wait_send()
     store_gg.wait()
     store_gf.wait()
-    store_gi.wait()
 
 
 def store_results(*refs):
@@ -506,7 +542,6 @@
         slab(32),
         slab(32),
         pltpu.VMEM((2, SHARDS, 16, LANES), F32),
-        pltpu.VMEM((SHARDS, 2, 16, LANES), F32),
         pltpu.VMEM((2, 3, 2, LANES, WIDE), F32),
         pltpu.VMEM((2, 2, LANES, WIDE), F32),
         pltpu.VMEM((2, LANES, WIDE), F32),
@@ -514,11 +549,11 @@
         pltpu.VMEM((2 * SHARDS, 2, 8, LANES), F32),
         slab(8),
         slab(8),
-        pltpu.VMEM((8, SHARDS, 8, LANES), F32),
+        pltpu.VMEM((2, 4, SHARDS, 8, LANES), F32),
         pltpu.VMEM((1024, LANES), F32),
         pltpu.SemaphoreType.DMA((9,)),
-        pltpu.SemaphoreType.DMA((14,)),
-        pltpu.SemaphoreType.DMA((14,)),
+        pltpu.SemaphoreType.DMA((16,)),
+        pltpu.SemaphoreType.DMA((16,)),
     ]
     in_hbm = pl.BlockSpec(memory_space=pltpu.HBM)
     anywhere = pl.BlockSpec(memory_space=pl.ANY)

time: 59.4 us -> 61.5 us (1.035)
  Pallas kernels: 58.6 us -> 60.8 us
    pallas_call x1, Pallas kernels: 57.6 us -> 59.8 us  [per_device(): pl.pallas_call(kernel, out_shape=results, in_specs=[in_hbm] * len(operand...]
where the time goes in v4:
time: 61.5 us; the launch traced here: 61.4 us
  Pallas kernels  60.8 us (99%)
  between operations  0.64 us (1%)
    pallas_call x1, Pallas kernels, per_device(): pl.pallas_call(kernel, out_shape=results, in_specs=[in_hbm] * len(operand...  59.8 us

profile of v4, /device:TPU:1, one launch (start us, length us, event | category | flops | bytes accessed | tf_op | source)
XLA Modules:
  0.0 61.4 jit_solution(5271087324136666662)
XLA Ops:
  0.6 59.8 %gated_conv_back.1 = (f32[16,2,16,128]{3,2,1,0:T(8,128)S(1)}, f32[512,128]{1,0:T(8,128)S(1)}, f32[1024,128]{1,0:T(8,128)S(1)}) custom-call(f32[512,128]{1,0:T(8,128)} %bitcast.37, f32[512,128]{1,0:T(8,128)} %bitcast.38, f32[2,2,512,128]{3,2,1,0:T(8,128)} %bitcast.36, f32[2,4,512,128]{3,2,1,0:T(8,128)} %bitcast.35, ...), custom_call_target="tpu_custom_call" | custom-call | tf_op jit(solution)/shard_map/gated_conv_back/pallas_call | solution.py:565
  60.4 1.0 %store_results.1 = (f32[16,2,16,128]{3,2,1,0:T(8,128)}, f32[512,128]{1,0:T(8,128)}, f32[1024,128]{1,0:T(8,128)}) custom-call(f32[16,2,16,128]{3,2,1,0:T(8,128)S(1)} %get-tuple-element.9.refs_0_, f32[512,128]{1,0:T(8,128)S(1)} %get-tuple-element.10.refs_1_, f32[1024,128]{1,0:T(8,128)S(1)} %get-tuple-element.11.refs_2_), custom_call_target="tpu_custom_call" | custom-call | tf_op jit(solution)/shard_map/store_results/pallas_call | solution.py:576

commit v5 on v4

--- a/solution.py
+++ b/solution.py
@@ -162,6 +162,13 @@
     other = group + 1 - 2 * core
     peers = [(me // 4 + dx) % 4 * 4 + (me + dz) % 4 for dx, dz in STEPS]
 
+    def load(k, src, dst):
+        copy = pltpu.make_async_copy(src, dst, load_sem.at[k])
+        copy.start()
+        return copy
+
+    loads = [load(0, grad_hbm, grad), load(1, gate_hbm, gate)]
+
     barrier = pltpu.get_barrier_semaphore()
     for peer in peers:
         pl.semaphore_signal(barrier, inc=1, device_id={"ctx": peer}, device_id_type=MESH)
@@ -172,14 +179,7 @@
             pl.semaphore_signal(barrier, inc=1, device_id={"ch": there}, device_id_type=MESH)
     pl.semaphore_signal(barrier, inc=1, device_id={"ch": other}, device_id_type=MESH)
 
-    def load(k, src, dst):
-        copy = pltpu.make_async_copy(src, dst, load_sem.at[k])
-        copy.start()
-        return copy
-
-    loads = [
-        load(0, grad_hbm, grad),
-        load(1, gate_hbm, gate),
+    loads += [
         load(2, inner_hbm, inner),
         load(3, lane_rows_hbm, lane_rows),
         load(4, picked_hbm, picked),
@@ -197,6 +197,16 @@
             ).start()
         into[me] = out[me]
 
+    def send_piece(k, out, into, b, half):
+        for peer in peers:
+            pltpu.make_async_remote_copy(
+                out.at[b, peer, half], into.at[b, me, half], send_sem.at[k], recv_sem.at[k],
+                device_id={"ctx": peer}, device_id_type=MESH,
+            ).start()
+
+    def piece(ref, b, half):
+        return ref.at[b, pl.ds(0, SHARDS - 1), half]
+
     def bulk(k, ref):
         return pltpu.make_async_remote_copy(
             ref, ref, send_sem.at[k], recv_sem.at[k], device_id={"ctx": (me + 1) % SHARDS}, device_id_type=MESH
@@ -211,6 +221,9 @@
     loads[0].wait()
     loads[1].wait()
     x_out[...] = (grad[...] * gate[...]).reshape(SHARDS, 32, LANES)
+
+    pl.semaphore_wait(barrier, 2 * SHARDS - 1 + 6)
+    send_all(0, x_out, x_in)
 
     for k in (2, 3, 4):
         loads[k].wait()
@@ -257,9 +270,12 @@
             out.append((sr * pr + si * pi, si * pr - sr * pi))
         return out
 
-    pl.semaphore_wait(barrier, 2 * SHARDS - 1 + 6)
-
-    send_all(0, x_out, x_in)
+    def put_row(out, b, arrays):
+        for ch, both in enumerate(inverse_rows(b, arrays)):
+            for ri in range(2):
+                pieces = both[ri].reshape(SHARDS, 16, LANES)
+                for half in range(2):
+                    out[b, :, half, ri, ch] = pieces[:, 8 * half : 8 * half + 8]
 
     def conv_row(b):
         hr, hi = prods[b, 0, 0], prods[b, 0, 1]
@@ -267,9 +283,7 @@
         for ch in range(2):
             ur, ui = prods[b, 1 + ch, 0], prods[b, 1 + ch, 1]
             arrays.append((ur * hr - ui * hi, ur * hi + ui * hr))
-        for ch, (re, im) in enumerate(inverse_rows(b, arrays)):
-            c_out[b, :, 0, ch] = re.reshape(SHARDS, 16, LANES)
-            c_out[b, :, 1, ch] = im.reshape(SHARDS, 16, LANES)
+        put_row(c_out, b, arrays)
 
     def slab_forward(step, carry):
         ch, half = step // 2, step % 2
@@ -291,12 +305,14 @@
 
         @pl.when(step == 0)
         def _():
-            send_all(3, c_out.at[0], c_in.at[0])
+            send_piece(3, c_out, c_in, 0, 0)
+            c_in[0, me] = c_out[0, me]
             arrived(0, x_in)
             lax.fori_loop(0, 4, slab_forward, 0)
             for turn in range(2):
                 b = (1 - core + turn) % 2
                 send_all(1 + turn, y_out.at[b], y_in.at[b])
+            send_piece(16, c_out, c_in, 0, 1)
 
         return carry
 
@@ -333,11 +349,7 @@
 
     def input_row(b):
         arrays = [(prods[b, 1 + ch, 0], prods[b, 1 + ch, 1]) for ch in range(2)]
-        for ch, both in enumerate(inverse_rows(b, arrays)):
-            for ri in range(2):
-                pieces = both[ri].reshape(SHARDS, 16, LANES)
-                for half in range(2):
-                    i_out[b, :, half, ri, ch] = pieces[:, 8 * half : 8 * half + 8]
+        put_row(i_out, b, arrays)
 
     def filter_row():
         swap.wait_recv()
@@ -366,22 +378,16 @@
         @pl.when(turn == 1)
         def _():
             filter_row()
+            send_piece(7, i_out, i_in, 1 - core, 0)
 
         input_row(b)
 
-        @pl.when(turn == 0)
-        def _():
-            send_all(7, i_out.at[1 - core], i_in.at[1 - core])
-
         return carry
 
     lax.fori_loop(0, 2, row_turn, 0)
-    for peer in peers:
-        pltpu.make_async_remote_copy(
-            i_out.at[core, peer, 0], i_in.at[core, me, 0], send_sem.at[8], recv_sem.at[8],
-            device_id={"ctx": peer}, device_id_type=MESH,
-        ).start()
-    i_in[core, me] = i_out[core, me]
+    send_piece(8, i_out, i_in, core, 0)
+    i_in[0, me] = i_out[0, me]
+    i_in[1, me] = i_out[1, me]
 
     def slab_back(row, put):
         ws = [None] * RADIX
@@ -401,34 +407,25 @@
             put(j, 1, im)
 
     def conv_back(half, carry):
-        at = pl.ds(pl.multiple_of(8 * half, 8), 8)
-
         def put(j, ch, value):
             d_out[j, pl.ds(16 * half + ch, 8, stride=2), :] = value
 
-        slab_back(lambda r, ri, ch: c_in[r % 2, r // 2, ri, ch, at, :], put)
+        slab_back(lambda r, ri, ch: c_in[r % 2, r // 2, half, ri, ch], put)
         return carry
 
-    arrived(3, c_in.at[0])
+    bulk(3, piece(c_in, 0, 0)).wait_recv()
+    bulk(16, piece(c_in, 0, 1)).wait_recv()
     arrived(4, c_in.at[1])
     lax.fori_loop(0, 2, conv_back, 0)
-    send_all(9, d_out, d_in)
 
     bulk(6, f_in.at[pl.ds(0, 2 * SHARDS - 1)]).wait_recv()
     ws = [(f_in[r, 0], f_in[r, 1]) for r in range(RADIX)]
     for j, (re, _) in enumerate(back_dft(ws, first_half=True)):
         g_out[j] = re + re
     send_all(10, g_out, g_in)
-    for peer in peers:
-        pltpu.make_async_remote_copy(
-            i_out.at[core, peer, 1], i_in.at[core, me, 1], send_sem.at[15], recv_sem.at[15],
-            device_id={"ctx": peer}, device_id_type=MESH,
-        ).start()
-
-    arrived(7, i_in.at[1 - core])
-
-    def half_of(ref, half):
-        return ref.at[core, pl.ds(0, SHARDS - 1), half]
+    send_piece(15, i_out, i_in, 1 - core, 1)
+    send_piece(17, i_out, i_in, core, 1)
+    send_all(9, d_out, d_in)
 
     share = pltpu.make_async_remote_copy(
         g_all.at[core], g_all.at[core], send_sem.at[14], recv_sem.at[14],
@@ -436,7 +433,8 @@
     )
 
     def input_back(half, carry):
-        bulk(8 + 7 * half, half_of(i_in, half)).wait_recv()
+        bulk(7 + 8 * half, piece(i_in, 1 - core, half)).wait_recv()
+        bulk(8 + 9 * half, piece(i_in, core, half)).wait_recv()
 
         def put(j, ch, value):
             e_out[half, j, pl.ds(ch, 8, stride=2), :] = value
@@ -485,12 +483,13 @@
     left(0, x_out)
     for turn in range(2):
         left(1 + turn, y_out.at[turn])
-        left(3 + turn, c_out.at[turn])
-        bulk(8 + 7 * turn, half_of(i_out, turn)).wait_send()
+        bulk(3 + 13 * turn, piece(c_out, 0, turn)).wait_send()
+        bulk(7 + 8 * turn, piece(i_out, 1 - core, turn)).wait_send()
+        bulk(8 + 9 * turn, piece(i_out, core, turn)).wait_send()
         left(11 + turn, e_out.at[turn])
     swap.wait_send()
     bulk(6, f_out.at[pl.ds(0, 2 * SHARDS - 1)]).wait_send()
-    left(7, i_out.at[1 - core])
+    left(4, c_out.at[1])
     left(9, d_out)
     left(10, g_out)
     bulk(13, g_all.at[core, pl.ds(0, 3)]).wait_send()
@@ -535,8 +534,8 @@
         slab(32),
         wave,
         wave,
-        wave,
-        wave,
+        half_wave,
+        half_wave,
         half_wave,
         half_wave,
         slab(32),
@@ -552,8 +551,8 @@
         pltpu.VMEM((2, 4, SHARDS, 8, LANES), F32),
         pltpu.VMEM((1024, LANES), F32),
         pltpu.SemaphoreType.DMA((9,)),
-        pltpu.SemaphoreType.DMA((16,)),
-        pltpu.SemaphoreType.DMA((16,)),
+        pltpu.SemaphoreType.DMA((18,)),
+        pltpu.SemaphoreType.DMA((18,)),
     ]
     in_hbm = pl.BlockSpec(memory_space=pltpu.HBM)
     anywhere = pl.BlockSpec(memory_space=pl.ANY)

time: 61.5 us -> 59.3 us (0.964); the launches traced: 61.4 us -> 58.3 us
  Pallas kernels: 60.8 us -> 57.6 us
    pallas_call x1, Pallas kernels: 59.8 us -> 56.6 us  [per_device(): pl.pallas_call(kernel, out_shape=results, in_specs=[in_hbm] * len(operand...]
where the time goes in v5:
time: 59.3 us; the launch traced here: 58.3 us
  Pallas kernels  57.6 us (97%)
  between operations  0.64 us (1%)
    pallas_call x1, Pallas kernels, per_device(): pl.pallas_call(kernel, out_shape=results, in_specs=[in_hbm] * len(operand...  56.6 us

profile of v5, /device:TPU:1, one launch (start us, length us, event | category | flops | bytes accessed | tf_op | source)
XLA Modules:
  0.0 58.3 jit_solution(2906447070268176269)
XLA Ops:
  0.6 56.6 %gated_conv_back.1 = (f32[16,2,16,128]{3,2,1,0:T(8,128)S(1)}, f32[512,128]{1,0:T(8,128)S(1)}, f32[1024,128]{1,0:T(8,128)S(1)}) custom-call(f32[512,128]{1,0:T(8,128)} %bitcast.37, f32[512,128]{1,0:T(8,128)} %bitcast.38, f32[2,2,512,128]{3,2,1,0:T(8,128)} %bitcast.36, f32[2,4,512,128]{3,2,1,0:T(8,128)} %bitcast.35, ...), custom_call_target="tpu_custom_call" | custom-call | tf_op jit(solution)/shard_map/gated_conv_back/pallas_call | solution.py:564
  57.3 1.0 %store_results.1 = (f32[16,2,16,128]{3,2,1,0:T(8,128)}, f32[512,128]{1,0:T(8,128)}, f32[1024,128]{1,0:T(8,128)}) custom-call(f32[16,2,16,128]{3,2,1,0:T(8,128)S(1)} %get-tuple-element.9.refs_0_, f32[512,128]{1,0:T(8,128)S(1)} %get-tuple-element.10.refs_1_, f32[1024,128]{1,0:T(8,128)S(1)} %get-tuple-element.11.refs_2_), custom_call_target="tpu_custom_call" | custom-call | tf_op jit(solution)/shard_map/store_results/pallas_call | solution.py:575

commit v6 on v5

--- a/solution.py
+++ b/solution.py
@@ -500,7 +500,12 @@
 
 def store_results(*refs):
     ins, outs, sem = refs[:3], refs[3:6], refs[6]
-    copies = [pltpu.make_async_copy(src, dst, sem.at[k]) for k, (src, dst) in enumerate(zip(ins, outs))]
+    copies = []
+    for src, dst in zip(ins, outs):
+        step = src.shape[0] // 4
+        for k in range(4):
+            rows = pl.ds(k * step, step)
+            copies.append(pltpu.make_async_copy(src.at[rows], dst.at[rows], sem.at[len(copies)]))
     for copy in copies:
         copy.start()
     for copy in copies:
@@ -577,7 +582,7 @@
         out_shape=results,
         in_specs=[anywhere] * 3,
         out_specs=[in_hbm] * 3,
-        scratch_shapes=[pltpu.SemaphoreType.DMA((3,))],
+        scratch_shapes=[pltpu.SemaphoreType.DMA((12,))],
         compiler_params=pltpu.CompilerParams(vmem_limit_bytes=2**20),
         name="store_results",
     )(*found)

time: 59.3 us -> 59.3 us (level)
  no operation moved by 1% of the time
where the time goes in v6:
time: 59.3 us; the launch traced here: 58.3 us
  Pallas kernels  57.7 us (97%)
  between operations  0.64 us (1%)
    pallas_call x1, Pallas kernels, per_device(): pl.pallas_call(kernel, out_shape=results, in_specs=[in_hbm] * len(operand...  56.6 us

profile of v6, /device:TPU:1, one launch (start us, length us, event | category | flops | bytes accessed | tf_op | source)
XLA Modules:
  0.0 58.3 jit_solution(5358355866809355374)
XLA Ops:
  0.6 56.6 %gated_conv_back.1 = (f32[16,2,16,128]{3,2,1,0:T(8,128)S(1)}, f32[512,128]{1,0:T(8,128)S(1)}, f32[1024,128]{1,0:T(8,128)S(1)}) custom-call(f32[512,128]{1,0:T(8,128)} %bitcast.37, f32[512,128]{1,0:T(8,128)} %bitcast.38, f32[2,2,512,128]{3,2,1,0:T(8,128)} %bitcast.36, f32[2,4,512,128]{3,2,1,0:T(8,128)} %bitcast.35, ...), custom_call_target="tpu_custom_call" | custom-call | tf_op jit(solution)/shard_map/gated_conv_back/pallas_call | solution.py:569
  57.3 1.1 %store_results.1 = (f32[16,2,16,128]{3,2,1,0:T(8,128)}, f32[512,128]{1,0:T(8,128)}, f32[1024,128]{1,0:T(8,128)}) custom-call(f32[16,2,16,128]{3,2,1,0:T(8,128)S(1)} %get-tuple-element.9.refs_0_, f32[512,128]{1,0:T(8,128)S(1)} %get-tuple-element.10.refs_1_, f32[1024,128]{1,0:T(8,128)S(1)} %get-tuple-element.11.refs_2_), custom_call_target="tpu_custom_call" | custom-call | tf_op jit(solution)/shard_map/store_results/pallas_call | solution.py:580
